TPU v7x, 32 devices: a whole 2x2x4 slice. The times are simulated.
32 devices in a mesh: ctx: 8 (over y, x, core), fsdp: 4 (over z).
Axes of the slice: x: 2, y: 2, z: 4, core: 2. Of those that a mesh axis runs over, the one named last changes fastest.
Arguments:
- layer_input: bfloat16 [4, 1024, 960], P('fsdp', 'ctx'), may hold values from -60 to 60
- output_grad: bfloat16 [4, 1024, 960], P('fsdp', 'ctx'), may hold values from -6 to 6
- query_weight: bfloat16 [960, 960], P('fsdp'), may hold values from -0.1875 to 0.1875
- key_weight: bfloat16 [960, 320], P('fsdp'), may hold values from -0.1875 to 0.1875
- value_weight: bfloat16 [960, 320], P('fsdp'), may hold values from -0.1875 to 0.1875
- output_weight: bfloat16 [960, 960], P('fsdp'), may hold values from -6 to 6
- gate_weight: bfloat16 [960, 2560], P('fsdp'), may hold values from -0.1875 to 0.1875
- up_weight: bfloat16 [960, 2560], P('fsdp'), may hold values from -0.1875 to 0.1875
- down_weight: bfloat16 [2560, 960], P('fsdp'), may hold values from -0.125 to 0.125
- norm_gains: float32 [2, 960], replicated, may hold values from 0.5 to 1.5
- query_momentum: float32 [960, 960], P('fsdp'), may hold values from -160 to 160
- key_momentum: float32 [960, 320], P('fsdp'), may hold values from -384 to 384
- value_momentum: float32 [960, 320], P('fsdp'), may hold values from -384 to 384
- output_momentum: float32 [960, 960], P('fsdp'), may hold values from -40 to 40
- gate_momentum: float32 [960, 2560], P('fsdp'), may hold values from -80 to 80
- up_momentum: float32 [960, 2560], P('fsdp'), may hold values from -80 to 80
- down_momentum: float32 [2560, 960], P('fsdp'), may hold values from -80 to 80
- gain_momentum: float32 [2, 960], P(None, 'fsdp'), may hold values from -1024 to 1024
- block_order: int32 [16], replicated, may hold values from 0 to 15, each once
Outputs:
- layer_output: bfloat16 [4, 1024, 960], P('fsdp', 'ctx')
- input_gradient: float32 [4, 1024, 960], P('fsdp', 'ctx')
- query_gradient: float32 [960, 960], P('fsdp')
- key_gradient: float32 [960, 320], P('fsdp')
- value_gradient: float32 [960, 320], P('fsdp')
- output_gradient: float32 [960, 960], P('fsdp')
- gate_gradient: float32 [960, 2560], P('fsdp')
- up_gradient: float32 [960, 2560], P('fsdp')
- down_gradient: float32 [2560, 960], P('fsdp')
- gain_gradient: float32 [2, 960], P(None, 'fsdp')
- new_query_momentum: float32 [960, 960], P('fsdp')
- new_key_momentum: float32 [960, 320], P('fsdp')
- new_value_momentum: float32 [960, 320], P('fsdp')
- new_output_momentum: float32 [960, 960], P('fsdp')
- new_gate_momentum: float32 [960, 2560], P('fsdp')
- new_up_momentum: float32 [960, 2560], P('fsdp')
- new_down_momentum: float32 [2560, 960], P('fsdp')
- new_gain_momentum: float32 [2, 960], P(None, 'fsdp')
- new_query_weight: float32 [960, 960], P('fsdp')
- new_key_weight: float32 [960, 320], P('fsdp')
- new_value_weight: float32 [960, 320], P('fsdp')
- new_output_weight: float32 [960, 960], P('fsdp')
- new_gate_weight: float32 [960, 2560], P('fsdp')
- new_up_weight: float32 [960, 2560], P('fsdp')
- new_down_weight: float32 [2560, 960], P('fsdp')
- new_norm_gains: float32 [2, 960], P(None, 'fsdp')
Inputs may be any that keep to these rules, and one draw needn't show every extreme that they name: `block_order`: every block of a sequence stands in exactly one slot.
All inputs are finite; a program needn't handle non-finite values.
Results may differ from a plain program's by a relative error of at most 0.017.
Values may be sent and summed in bfloat16 or wider, within the bound.
A program may use at most 448 MiB of HBM per device.

v0:
```python
import math

import jax
import jax.numpy as jnp
from jax import lax
from jax.sharding import PartitionSpec as P

HEADS = 15
KV_HEADS = 5
HEAD = 64
NS_ITERS = 5


EPS = 1e-05
THETA = 100000.0
NS_A = 3.4445
NS_B = -4.775
NS_C = 2.0315
MOMENTUM = 0.95
RATE = 0.2
OUT_RATE = 6.0
GAIN_RATE = 0.002
MASKED = -1e30


def as_sent(array):

    def short(part):
        return part.astype(jnp.bfloat16) if part.dtype == jnp.float32 else part

    return jax.tree.map(short, array)


def contract(left, right, left_dim, right_dim):
    return lax.dot_general(
        left, right, (((left_dim,), (right_dim,)), ((), ())), preferred_element_type=jnp.float32
    )


def rotary_tables(positions, width):
    half = width // 2
    frequency = THETA ** (-(jnp.arange(half, dtype=jnp.float32) * 2.0 / width))
    angle = positions.astype(jnp.float32)[:, None] * frequency[None, :]
    return (jnp.cos(angle)[:, None, :], jnp.sin(angle)[:, None, :])


def rotate(value, cosine, sine):
    half = value.shape[-1] // 2
    first = value[..., :half]
    second = value[..., half:]
    return jnp.concatenate(
        [first * cosine - second * sine, second * cosine + first * sine], axis=-1
    )


def unrotate(incoming, cosine, sine):
    half = incoming.shape[-1] // 2
    upper = incoming[..., :half]
    lower = incoming[..., half:]
    return jnp.concatenate([upper * cosine + lower * sine, lower * cosine - upper * sine], axis=-1)


def norm_forward(residual, gain):
    inverse = lax.rsqrt(jnp.mean(residual * residual, axis=-1, keepdims=True) + EPS)
    return ((residual * inverse * gain).astype(jnp.bfloat16), inverse)


def norm_backward(residual, inverse, gain, incoming):
    scaled = incoming * gain
    through = inverse * scaled - residual * inverse**3 * jnp.mean(
        scaled * residual, axis=-1, keepdims=True
    )
    return (through, jnp.sum(incoming * residual * inverse, axis=0))


def iterate_step(current, gram):
    gram = lax.optimization_barrier(gram)
    poly = (
        NS_B * gram.astype(jnp.float32)
        + NS_C * jnp.dot(gram, gram, preferred_element_type=jnp.float32)
    ).astype(jnp.bfloat16)
    current = lax.optimization_barrier(current)
    return (
        NS_A * current.astype(jnp.float32)
        + jnp.dot(poly, current, preferred_element_type=jnp.float32)
    ).astype(jnp.bfloat16)


def newton_schulz(matrix):
    flip = matrix.shape[0] > matrix.shape[1]
    oriented = matrix.T if flip else matrix
    wide = oriented.astype(jnp.float32)
    scale = jnp.sqrt(jnp.sum(wide * wide))
    current = (wide / (scale + 1e-07)).astype(jnp.bfloat16)
    for count in range(NS_ITERS):
        current = iterate_step(current, contract(current, current, 1, 1).astype(jnp.bfloat16))
    return current.T if flip else current


def split_flat(flat, templates):
    pieces = []
    offset = 0
    for template in templates:
        pieces.append(flat[offset : offset + template.size].reshape(template.shape))
        offset += template.size
    return pieces


def pack_line(pieces, width_slot):
    filled = sum((piece.shape[-1] for piece in pieces))
    lead = pieces[0].shape[:-1] if pieces else ()
    chosen = list(pieces)
    if width_slot > filled:
        chosen.append(jnp.zeros(lead + (width_slot - filled,), jnp.bfloat16))
    return jnp.concatenate(chosen, axis=-1) if len(chosen) > 1 else chosen[0]


def on_device(
    layer_input,
    output_grad,
    query_weight,
    key_weight,
    value_weight,
    output_weight,
    gate_weight,
    up_weight,
    down_weight,
    norm_gains,
    query_momentum,
    key_momentum,
    value_momentum,
    output_momentum,
    gate_momentum,
    up_momentum,
    down_momentum,
    gain_momentum,
    block_order,
):
    rows = layer_input.shape[1]
    block = rows // 2
    group = HEADS // KV_HEADS
    scale = 1.0 / math.sqrt(HEAD)
    ctx_size = lax.axis_size("ctx")
    parts = lax.axis_size("fsdp")
    ctx_place = lax.axis_index("ctx")
    offsets = jnp.arange(block, dtype=jnp.int32)
    own_blocks = lax.dynamic_slice_in_dim(block_order, 2 * ctx_place, 2)
    query_pos = (own_blocks[:, None] * block + offsets[None, :]).reshape(rows)
    key_pos = (block_order[:, None] * block + offsets[None, :]).reshape(-1)
    full = (
        lax.all_gather(query_weight, "fsdp", axis=0, tiled=True),
        lax.all_gather(key_weight, "fsdp", axis=0, tiled=True),
        lax.all_gather(value_weight, "fsdp", axis=0, tiled=True),
        lax.all_gather(output_weight, "fsdp", axis=0, tiled=True),
        lax.all_gather(gate_weight, "fsdp", axis=0, tiled=True),
        lax.all_gather(up_weight, "fsdp", axis=0, tiled=True),
        lax.all_gather(down_weight, "fsdp", axis=0, tiled=True),
    )
    full_query, full_key, full_value, full_output, full_gate, full_up, full_down = full
    residual = layer_input[0].astype(jnp.float32)
    normed_first, inverse_first = norm_forward(residual, norm_gains[0])
    query_pre = jnp.dot(normed_first, full_query, preferred_element_type=jnp.float32).reshape(
        rows, HEADS, HEAD
    )
    key_pre = jnp.dot(normed_first, full_key, preferred_element_type=jnp.float32).reshape(
        rows, KV_HEADS, HEAD
    )
    value_low = (
        jnp.dot(normed_first, full_value, preferred_element_type=jnp.float32)
        .astype(jnp.bfloat16)
        .reshape(rows, KV_HEADS, HEAD)
    )
    cosine, sine = rotary_tables(query_pos, HEAD)
    query_rot = rotate(query_pre, cosine, sine).astype(jnp.bfloat16)
    key_rot = rotate(key_pre, cosine, sine).astype(jnp.bfloat16)
    keys_all, values_all = (
        lax.all_gather(key_rot, "ctx", axis=0, tiled=True),
        lax.all_gather(value_low, "ctx", axis=0, tiled=True),
    )
    keys_head = keys_all.transpose(1, 0, 2)
    values_head = values_all.transpose(1, 0, 2)
    queries_head = (
        query_rot.reshape(rows, KV_HEADS, group, HEAD)
        .transpose(1, 2, 0, 3)
        .reshape(KV_HEADS, group * rows, HEAD)
    )
    row_pos = jnp.tile(query_pos, group)
    allowed = key_pos[None, :] <= row_pos[:, None]

    def head_forward(item):
        query, key, value = item
        scores = jnp.where(allowed, contract(query, key, 1, 1) * scale, MASKED)
        top = jnp.max(scores, axis=-1, keepdims=True)
        expo = jnp.exp(scores - top)
        total = jnp.sum(expo, axis=-1, keepdims=True)
        probs_low = (expo / total).astype(jnp.bfloat16)
        return (
            jnp.dot(probs_low, value, preferred_element_type=jnp.float32),
            (top + jnp.log(total))[:, 0],
        )

    mixed, log_total = lax.map(head_forward, (queries_head, keys_head, values_head))
    attended = (
        mixed.reshape(KV_HEADS, group, rows, HEAD)
        .transpose(2, 0, 1, 3)
        .reshape(rows, HEADS * HEAD)
        .astype(jnp.bfloat16)
    )
    middle = residual + jnp.dot(attended, full_output, preferred_element_type=jnp.float32)
    normed_second, inverse_second = norm_forward(middle, norm_gains[1])
    gate = jnp.dot(normed_second, full_gate, preferred_element_type=jnp.float32)
    lifted = jnp.dot(normed_second, full_up, preferred_element_type=jnp.float32)
    sigma = jax.nn.sigmoid(gate)
    hidden = (gate * sigma * lifted).astype(jnp.bfloat16)
    layer_output = (middle + jnp.dot(hidden, full_down, preferred_element_type=jnp.float32)).astype(
        jnp.bfloat16
    )
    upstream = output_grad[0]
    grad_hidden = contract(upstream, full_down, 1, 1)
    grad_gate = (grad_hidden * lifted * sigma * (1.0 + gate * (1.0 - sigma))).astype(jnp.bfloat16)
    grad_lifted = (grad_hidden * gate * sigma).astype(jnp.bfloat16)
    grad_normed_second = contract(grad_gate, full_gate, 1, 1) + contract(grad_lifted, full_up, 1, 1)
    through_second, gain_second = norm_backward(
        middle, inverse_second, norm_gains[1], grad_normed_second
    )
    grad_middle = upstream.astype(jnp.float32) + through_second
    grad_branch = grad_middle.astype(jnp.bfloat16)
    grad_attended = contract(grad_branch, full_output, 1, 1).astype(jnp.bfloat16)
    grad_heads = (
        grad_attended.reshape(rows, KV_HEADS, group, HEAD)
        .transpose(1, 2, 0, 3)
        .reshape(KV_HEADS, group * rows, HEAD)
    )

    def head_backward(item):
        query, key, value, grad_out, log_row = item
        scores = jnp.where(allowed, contract(query, key, 1, 1) * scale, MASKED)
        probs = jnp.exp(scores - log_row[:, None])
        grad_value_part = contract(probs.astype(jnp.bfloat16), grad_out, 0, 0)
        grad_probs = contract(grad_out, value, 1, 1)
        grad_scores = (
            probs * (grad_probs - jnp.sum(grad_probs * probs, axis=-1, keepdims=True))
        ).astype(jnp.bfloat16)
        grad_query_part = jnp.dot(grad_scores, key, preferred_element_type=jnp.float32) * scale
        grad_key_part = contract(grad_scores, query, 0, 0) * scale
        return (grad_query_part, grad_key_part, grad_value_part)

    grad_query_rot, grad_key_all, grad_value_all = lax.map(
        head_backward, (queries_head, keys_head, values_head, grad_heads, log_total)
    )
    grad_key_own, grad_value_own = (
        lax.psum_scatter(
            grad_key_all.astype(jnp.bfloat16), "ctx", scatter_dimension=1, tiled=True
        ).astype(jnp.float32),
        lax.psum_scatter(
            grad_value_all.astype(jnp.bfloat16), "ctx", scatter_dimension=1, tiled=True
        ).astype(jnp.float32),
    )
    grad_query = (
        unrotate(
            grad_query_rot.reshape(KV_HEADS, group, rows, HEAD)
            .transpose(2, 0, 1, 3)
            .reshape(rows, HEADS, HEAD),
            cosine,
            sine,
        )
        .reshape(rows, HEADS * HEAD)
        .astype(jnp.bfloat16)
    )
    grad_key = (
        unrotate(grad_key_own.transpose(1, 0, 2), cosine, sine)
        .reshape(rows, KV_HEADS * HEAD)
        .astype(jnp.bfloat16)
    )
    grad_value = (
        grad_value_own.transpose(1, 0, 2).reshape(rows, KV_HEADS * HEAD).astype(jnp.bfloat16)
    )
    grad_normed_first = (
        contract(grad_query, full_query, 1, 1)
        + contract(grad_key, full_key, 1, 1)
        + contract(grad_value, full_value, 1, 1)
    )
    through_first, gain_first = norm_backward(
        residual, inverse_first, norm_gains[0], grad_normed_first
    )
    input_gradient = (grad_middle + through_first)[None]
    term_query = contract(normed_first, grad_query, 0, 0)
    term_key = contract(normed_first, grad_key, 0, 0)
    term_value = contract(normed_first, grad_value, 0, 0)
    term_output = contract(attended, grad_branch, 0, 0)
    term_gate = contract(normed_second, grad_gate, 0, 0)
    term_up = contract(normed_second, grad_lifted, 0, 0)
    term_down = contract(hidden, upstream, 0, 0)
    term_gains = jnp.stack([gain_first, gain_second], axis=1)
    olds = (
        query_momentum,
        key_momentum,
        value_momentum,
        output_momentum,
        gate_momentum,
        up_momentum,
        down_momentum,
        gain_momentum.T,
    )
    partials = (
        term_query,
        term_key,
        term_value,
        term_output,
        term_gate,
        term_up,
        term_down,
        term_gains,
    )
    flat = jnp.concatenate([term.reshape(parts, -1) for term in partials], axis=1)
    piece = flat.shape[1] // ctx_size
    arranged = (
        flat.reshape(parts, ctx_size, piece).transpose(1, 0, 2).reshape(ctx_size * parts, piece)
    )
    own_sum = lax.psum_scatter(arranged, ("ctx", "fsdp"), scatter_dimension=0, tiled=True)[0]
    old_flat = jnp.concatenate([old.reshape(-1) for old in olds])
    old_piece = lax.dynamic_slice_in_dim(old_flat, ctx_place * piece, piece)
    grad_flat, moment_flat = (
        lax.all_gather(own_sum.astype(jnp.bfloat16), "ctx", axis=0, tiled=True).astype(
            own_sum.dtype
        ),
        lax.all_gather(
            (MOMENTUM * old_piece + own_sum).astype(jnp.bfloat16), "ctx", axis=0, tiled=True
        ).astype(jnp.float32),
    )
    gradients = split_flat(grad_flat, olds)
    moments = split_flat(moment_flat, olds)
    shapes = [tuple(matrix.shape) for matrix in full]
    shard_sizes = [shape[0] * shape[1] // parts for shape in shapes]
    owners = [index % parts for index in range(len(shapes))]
    starts = []
    loads = [0] * parts
    for index in range(len(shapes)):
        starts.append(loads[owners[index]])
        loads[owners[index]] += shard_sizes[index]
    width_slot = max(loads)
    low_moments = [moments[index].astype(jnp.bfloat16).reshape(-1) for index in range(len(shapes))]
    outgoing = jnp.stack(
        [
            pack_line(
                [low_moments[index] for index in range(len(shapes)) if owners[index] == target],
                width_slot,
            )
            for target in range(parts)
        ]
    )
    incoming = lax.all_to_all(outgoing, "fsdp", split_axis=0, concat_axis=0, tiled=True)

    def owner_branch(target):

        def compute(received):
            results = []
            for index in range(len(shapes)):
                if owners[index] == target:
                    matrix = lax.slice_in_dim(
                        received, starts[index], starts[index] + shard_sizes[index], axis=1
                    ).reshape(shapes[index])
                    ortho = newton_schulz(matrix)
                    results.append(ortho.reshape(parts, shard_sizes[index]))
            if results:
                return pack_line(results, width_slot)
            return jnp.zeros((parts, width_slot), jnp.bfloat16)

        return compute

    orthogonal_rows = lax.switch(
        lax.axis_index("fsdp"), [owner_branch(target) for target in range(parts)], incoming
    )
    returned = jax.tree.map(
        lambda part, own: part.astype(own.dtype),
        lax.all_to_all(as_sent(orthogonal_rows), "fsdp", split_axis=0, concat_axis=0, tiled=True),
        orthogonal_rows,
    )
    old_weights = (
        query_weight,
        key_weight,
        value_weight,
        output_weight,
        gate_weight,
        up_weight,
        down_weight,
    )
    new_weights = []
    for index in range(len(shapes)):
        rows_full, cols_full = shapes[index]
        step_rate = OUT_RATE if index == 3 else RATE
        factor = -step_rate * max(1.0, cols_full / rows_full) ** 0.5
        shard = lax.slice_in_dim(
            returned[owners[index]], starts[index], starts[index] + shard_sizes[index], axis=0
        )
        new_weights.append(
            old_weights[index].astype(jnp.float32)
            + factor * shard.reshape(rows_full // parts, cols_full).astype(jnp.float32)
        )
    gain_width = norm_gains.shape[1] // parts
    gain_shard = lax.dynamic_slice_in_dim(
        norm_gains, lax.axis_index("fsdp") * gain_width, gain_width, 1
    )
    new_gains = gain_shard - GAIN_RATE * moments[7].T
    return (
        layer_output[None],
        input_gradient,
        gradients[0],
        gradients[1],
        gradients[2],
        gradients[3],
        gradients[4],
        gradients[5],
        gradients[6],
        gradients[7].T,
        moments[0],
        moments[1],
        moments[2],
        moments[3],
        moments[4],
        moments[5],
        moments[6],
        moments[7].T,
        new_weights[0],
        new_weights[1],
        new_weights[2],
        new_weights[3],
        new_weights[4],
        new_weights[5],
        new_weights[6],
        new_gains,
    )


def solution(mesh):
    return jax.shard_map(
        on_device,
        mesh=mesh,
        in_specs=(
            P("fsdp", "ctx", None),
            P("fsdp", "ctx", None),
            P("fsdp", None),
            P("fsdp", None),
            P("fsdp", None),
            P("fsdp", None),
            P("fsdp", None),
            P("fsdp", None),
            P("fsdp", None),
            P(),
            P("fsdp", None),
            P("fsdp", None),
            P("fsdp", None),
            P("fsdp", None),
            P("fsdp", None),
            P("fsdp", None),
            P("fsdp", None),
            P(None, "fsdp"),
            P(),
        ),
        out_specs=(
            P("fsdp", "ctx", None),
            P("fsdp", "ctx", None),
            P("fsdp", None),
            P("fsdp", None),
            P("fsdp", None),
            P("fsdp", None),
            P("fsdp", None),
            P("fsdp", None),
            P("fsdp", None),
            P(None, "fsdp"),
            P("fsdp", None),
            P("fsdp", None),
            P("fsdp", None),
            P("fsdp", None),
            P("fsdp", None),
            P("fsdp", None),
            P("fsdp", None),
            P(None, "fsdp"),
            P("fsdp", None),
            P("fsdp", None),
            P("fsdp", None),
            P("fsdp", None),
            P("fsdp", None),
            P("fsdp", None),
            P("fsdp", None),
            P(None, "fsdp"),
        ),
        check_vma=False,
    )
```

profile of v0, /device:TPU:0, one launch (start us, length us, event | category | flops | bytes accessed | tf_op | source)
XLA Modules:
  0.0 2566.7 jit_solution(2584870173491392865)
XLA Ops:
  12.2 25.6 all-gather
  49.7 23.8 all-gather.1
  126.7 81.0 %all-gather.12.cloned.1.call-done = bf16[960,2560]{1,0:T(8,128)(2,1)} async-done(((bf16[240,2560]{1,0:T(8,128)(2,1)}), bf16[960,2560]{1,0:T(8,128)(2,1)}) %all-gather.12.cloned.1.call-update) | async-done | bytes 4915216 | tf_op jit(solution)/shard_map/all_gather | solution.py:155
  212.1 88.2 %all-gather.14.cloned.1.call-done = bf16[960,2560]{1,0:T(8,128)(2,1)} async-done(((bf16[240,2560]{1,0:T(8,128)(2,1)}), bf16[960,2560]{1,0:T(8,128)(2,1)}) %all-gather.14.cloned.1.call-update) | async-done | bytes 4915216 | tf_op jit(solution)/shard_map/all_gather | solution.py:156
  304.6 88.2 %all-gather.16.cloned.1.call-done = bf16[2560,960]{0,1:T(8,128)(2,1)} async-done(((bf16[640,960]{0,1:T(8,128)(2,1)}), bf16[2560,960]{0,1:T(8,128)(2,1)}) %all-gather.16.cloned.1.call-update) | async-done | bytes 4915216 | tf_op jit(solution)/shard_map/all_gather | solution.py:157
  412.6 37.0 %while.31 = (s32[]{:T(128)}, f32[5,384,64]{1,2,0:T(8,128)S(1)}, bf16[5,1024,64]{1,2,0:T(8,128)(2,1)}, bf16[5,1024,64]{1,2,0:T(8,128)(2,1)}, bf16[5,384,64]{2,1,0...) while((s32[]{:T(128)}, f32[5,384,64]{1,2,0:T(8,128)S(1)}, ...), condition=%wide.region_9.10_spmd.clone.clone, body=%wide.region_7.9_spmd.clone.sunk.clone | while | flops 255680128 | bytes 13617273 | solution.py:248
  549.2 29.4 %reduce-scatter.9.cloned.1.call-done = bf16[128,320]{1,0:T(8,128)(2,1)} async-done(((bf16[1024,320]{1,0:T(8,128)(2,1)}), bf16[128,320]{1,0:T(8,128)(2,1)}) %reduce-scatter.9.cloned.1.call-update) | async-done | bytes 81936
  619.1 117.4 %reshape.686 = f32[9832320]{0:T(1024)} reshape(f32[4,2458080]{1,0:T(4,128)} %constant_dynamic-update-slice_fusion) | data formatting | bytes 78658560
  736.5 51.3 %reshape.589 = f32[4,8,307260]{2,1,0:T(8,128)} reshape(f32[9832320]{0:T(1024)} %reshape.686) | data formatting | bytes 78658560 | tf_op jit(solution)/shard_map/reshape | solution.py:318
  787.8 28.9 %copy.188 = f32[4,8,307260]{2,0,1:T(4,128)} copy(f32[4,8,307260]{2,1,0:T(8,128)} %reshape.589) | data formatting | bytes 78658560 | tf_op jit(solution)/shard_map/reshape | solution.py:318
  816.7 43.6 %reshape.590 = f32[32,307260]{1,0:T(8,128)} reshape(f32[8,4,307260]{2,1,0:T(4,128)} %bitcast.452) | data formatting | bytes 78658560 | tf_op jit(solution)/shard_map/reshape | solution.py:318
  879.2 555.6 %all-reduce.9.cloned.1.call-done = f32[32,307260]{1,0:T(8,128)} async-done(((f32[32,307260]{1,0:T(8,128)}), f32[32,307260]{1,0:T(8,128)}) %all-reduce.9.cloned.1.call-update) | async-done | bytes 39329296
  1474.3 142.6 %all-reduce.11.cloned.1.call-done = (bf16[2458080]{0:T(1024)(128)(2,1)}, bf16[2458080]{0:T(1024)(128)(2,1)}) async-done(((bf16[2458080]{0:T(1024)(128)(2,1)}, bf16[2458080]{0:T(1024)(128)(2,1)}), (bf16[2458080]{0:T(1024)(128)(2,1)}, bf16[2458080]{0:T(1024)(128)(2,1)})) %all-reduce.11.cloned.1.call-update) | async-done | bytes 9832336
  1621.5 19.3 stack.30
  1641.0 19.5 stack.29
  1660.5 19.3 stack.28
  1716.9 34.8 %reduce.42 = bf16[4,844800]{1,0:T(4,128)(2,1)} reduce(bf16[4,1,844800]{2,0,1:T(4,128)(2,1)} %maximum_bitcast_fusion, bf16[]{:T(256)} %broadcast.627), dimensions={1}, to_apply=%copy.159.reduce_sub_computation | reduce | bytes 13516802 | tf_op jit(solution)/shard_map/all_to_all | solution.py:352
  1788.6 125.8 %all-to-all-done = bf16[4,2,422400]{2,1,0:T(2,128)(2,1)} async-done(((bf16[4,2,422400]{2,1,0:T(2,128)(2,1)}), bf16[4,2,422400]{2,1,0:T(2,128)(2,1)}, u32[]{:S(2)}, u32[]{:S(2)}) %all-to-all-start) | async-done | bytes 6758432 | tf_op jit(solution)/shard_map/all_to_all | solution.py:352
  1935.1 293.1 %conditional.1 = (bf16[4,844800]{1,0:T(4,128)(2,1)}) conditional(s32[]{:T(128)} %clamp.3, bf16[4,844800]{1,0:T(4,128)(2,1)S(1)} %bitcast.448, bf16[4,844800]{1,0:T(4,128)(2,1)S(1)} %bitcast.449, bf16[4,844800]{1,0:T(4,128)(2,1)S(1)} %bitcast.450, bf16[4,844800]{1,0:T(4,128)(2,1)S(1)} %bitcast.451), branch_computations={%region_16.19_spmd, %region_19.22_spmd, %region_22.25_spmd, %regio... | conditional | flops 82732023808 | bytes 255590560 | solution.py:371
  2166.8 27.4 %pad_maximum_fusion = bf16[4,844800]{1,0:T(4,128)(2,1)} fusion(bf16[4,614400]{1,0:T(4,128)(2,1)} %reshape.531, bf16[4,230400]{1,0:T(4,128)(2,1)S(1)} %reshape.530), kind=kLoop, calls=%fused_computation.11 | loop fusion | flops 13516800 | bytes 13516800 | tf_op jit(solution)/shard_map/cond/branch_0_fun/concatenate | solution.py:115
  2228.2 34.8 %reduce.43 = bf16[4,844800]{1,0:T(4,128)(2,1)} reduce(bf16[4,1,844800]{2,0,1:T(4,128)(2,1)} %bitcast.457, bf16[]{:T(256)} %broadcast.627), dimensions={1}, to_apply=%copy.160.reduce_sub_computation | reduce | bytes 13516802 | tf_op jit(solution)/shard_map/all_to_all | solution.py:376
  2316.0 108.5 %all-to-all-done.1 = bf16[4,2,422400]{2,1,0:T(2,128)(2,1)} async-done(((bf16[4,2,422400]{2,1,0:T(2,128)(2,1)}), bf16[4,2,422400]{2,1,0:T(2,128)(2,1)}, u32[]{:S(2)}, u32[]{:S(2)}) %all-to-all-start.1) | async-done | bytes 6758432 | tf_op jit(solution)/shard_map/all_to_all | solution.py:376
  2453.0 34.3 %fusion.199 = (f32[614400]{0:T(1024)}, f32[614400]{0:T(1024)S(1)}) fusion(bf16[1,844800]{1,0:T(2,128)(2,1)S(1)} %get-tuple-element.381, bf16[1,844800]{1,0:T(2,128)(2,1)S(1)} %get-tuple-element.382), kind=kLoop, calls=%fused_computation.340 | loop fusion | flops 2457600 | bytes 7372800 | tf_op jit(solution)/shard_map/mul | solution.py:398
  2487.3 26.6 %fusion.203 = f32[614400]{0:T(1024)} fusion(bf16[1,844800]{1,0:T(2,128)(2,1)S(1)} %get-tuple-element.383), kind=kLoop, calls=%fused_computation.346 | loop fusion | flops 1228800 | bytes 3686400 | tf_op jit(solution)/shard_map/mul | solution.py:398
  (452 shorter events, 805.3 us)
Async XLA Ops:
  7.2 94.8 %all-gather.8.cloned.1.call-start = ((), (), s32[]{:S(2)}) async-start(), calls=%async_computation.4 | async-start | bytes 2457600 | tf_op jit(solution)/shard_map/all_gather | solution.py:151
  8.0 115.4 %all-gather.10.cloned.1.call-start = ((), (), s32[]{:S(2)}) async-start(), calls=%async_computation.5 | async-start | bytes 2457600 | tf_op jit(solution)/shard_map/all_gather | solution.py:154
  8.7 199.0 %all-gather.12.cloned.1.call-start = ((), (), s32[]{:S(2)}) async-start(), calls=%async_computation.6 | async-start | bytes 6144000 | tf_op jit(solution)/shard_map/all_gather | solution.py:155
  9.5 290.8 %all-gather.14.cloned.1.call-start = ((), (), s32[]{:S(2)}) async-start(), calls=%async_computation.7 | async-start | bytes 6144000 | tf_op jit(solution)/shard_map/all_gather | solution.py:156
  10.0 39.7 %copy-start.30 = (bf16[240,320]{0,1:T(8,128)(2,1)S(1)}, bf16[240,320]{0,1:T(8,128)(2,1)}, u32[]{:S(2)}) copy-start(bf16[240,320]{0,1:T(8,128)(2,1)} %param.31) | copy-start | bytes 460804
  10.1 382.8 %all-gather.16.cloned.1.call-start = ((), (), s32[]{:S(2)}) async-start(), calls=%async_computation.8 | async-start | bytes 6144000 | tf_op jit(solution)/shard_map/all_gather | solution.py:157
  10.6 534.5 %reduce-scatter.7.cloned.1.call-start = ((), (), s32[]{:S(2)}) async-start(), calls=%async_computation.9 | async-start | bytes 884736
  11.3 578.1 %copy-start.40 = (f32[1,960]{1,0:T(1,128)}, f32[1,960]{1,0:T(1,128)S(1)}, u32[]{:S(2)}) copy-start(f32[1,960]{1,0:T(1,128)S(1)} %get-tuple-element.421) | copy-start | bytes 11524
  12.0 62.6 %copy-start.43 = (f32[128]{0:T(128)}, f32[128]{0:T(128)S(1)}, u32[]{:S(2)}) copy-start(f32[128]{0:T(128)S(1)} %get-tuple-element.425) | copy-start | bytes 1540
  12.2 26.9 %copy-start.56 = (s32[128]{0:T(128)}, s32[128]{0:T(128)S(1)}, u32[]{:S(2)}) copy-start(s32[128]{0:T(128)S(1)} %add.406) | copy-start | bytes 1540
  39.1 49.1 %copy-start.35 = (f32[128,32]{0,1:T(8,128)}, f32[128,32]{0,1:T(8,128)S(1)}, u32[]{:S(2)}) copy-start(f32[128,32]{0,1:T(8,128)S(1)} %get-tuple-element.422) | copy-start | bytes 49156
  39.1 49.1 %copy-start.37 = (f32[128,32]{0,1:T(8,128)}, f32[128,32]{0,1:T(8,128)S(1)}, u32[]{:S(2)}) copy-start(f32[128,32]{0,1:T(8,128)S(1)} %get-tuple-element.423) | copy-start | bytes 49156
  74.6 16.4 copy-start.39
  123.2 84.6 %copy-start.49 = (s32[1024]{0:T(1024)}, s32[1024]{0:T(1024)S(1)}, u32[]{:S(2)}) copy-start(s32[1024]{0:T(1024)S(1)} %get-tuple-element.723) | copy-start | bytes 12292
  126.5 282.3 %copy-start.7 = (f32[128,960]{0,1:T(8,128)}, f32[128,960]{0,1:T(8,128)S(1)}, u32[]{:S(2)}) copy-start(f32[128,960]{0,1:T(8,128)S(1)} %get-tuple-element.429) | copy-start | bytes 1474564
  212.1 180.7 %copy-start.27 = (bf16[1,128,960]{1,2,0:T(8,128)(2,1)S(1)}, bf16[1,128,960]{1,2,0:T(8,128)(2,1)}, u32[]{:S(2)}) copy-start(bf16[1,128,960]{1,2,0:T(8,128)(2,1)} %param.28) | copy-start | bytes 737284
  459.3 119.3 %reduce-scatter.9.cloned.1.call-start = ((), (), s32[]{:S(2)}) async-start(), calls=%async_computation.10 | async-start | bytes 884736
  499.9 14.7 copy-start.19
  545.1 889.8 %all-reduce.9.cloned.1.call-start = ((), (), s32[]{:S(2)}) async-start(), calls=%async_computation.11 | async-start | bytes 78675968
  598.2 16.0 slice-start.3
  598.2 16.0 slice-start.4
  860.3 756.6 %all-reduce.11.cloned.1.call-start = ((), (), s32[]{:S(2)}) async-start(), calls=%async_computation.12 | async-start | bytes 19668992
  1759.9 154.5 %all-to-all-start = ((bf16[4,2,422400]{2,1,0:T(2,128)(2,1)}), bf16[4,2,422400]{2,1,0:T(2,128)(2,1)}, u32[]{:S(2)}, u32[]{:S(2)}) async-start(bf16[4,2,422400]{2,1,0:T(2,128)(2,1)} %reshape.688), calls=%async_computation | async-start | bytes 13516800 | tf_op jit(solution)/shard_map/all_to_all | solution.py:352
  2271.2 153.4 %all-to-all-start.1 = ((bf16[4,2,422400]{2,1,0:T(2,128)(2,1)}), bf16[4,2,422400]{2,1,0:T(2,128)(2,1)}, u32[]{:S(2)}, u32[]{:S(2)}) async-start(bf16[4,2,422400]{2,1,0:T(2,128)(2,1)} %reshape.690), calls=%async_computation.1 | async-start | bytes 13516800 | tf_op jit(solution)/shard_map/all_to_all | solution.py:376
  (55 other events, 351.0 us)
Sparse Core Ops, SparseCore 0:
  9.7 58.2 all-gather.7
  69.5 45.1 all-gather.9
  116.2 91.4 all-gather.11
  209.2 91.0 all-gather.13
  301.7 91.0 all-gather.15
  459.4 33.3 reduce-scatter.6
  545.2 33.4 reduce-scatter.8
  860.4 574.3 all-reduce.8
  1474.4 142.4 all-reduce.10
where the time goes:
time: 2580 us; the launch traced here: 2570 us
  waiting for transfers between devices  1220 us (47%)
  local copies, waits for them, and re-layouts  686 us (27%)
  matrix products  290 us (11%)
  other arithmetic  232 us (9%)
  blocking collectives  72.5 us (3%)
  loops' own time  36.2 us (1%)
    unnamed x13, waiting for transfers between devices  731 us
    unnamed x184, local copies, waits for them, and re-layouts  284 us
    dot_general x49, matrix products, contract(): lax.dot_general(left, right, (((left_dim,), (right_dim,)), ((), ())), pre...  152 us
    all_to_all x1, waiting for transfers between devices, on_device(): lax.all_to_all(outgoing, 'fsdp', split_axis=0, concat_axis=0, tiled=True)  126 us
    reshape x3, local copies, waits for them, and re-layouts, on_device(): flat.reshape(parts, ctx_size, piece).transpose(1, 0, 2)  124 us
    all_to_all x1, waiting for transfers between devices, on_device(): lax.all_to_all(as_sent(orthogonal_rows), 'fsdp', split_axis=0, concat_axi...  109 us
    dot_general x10, matrix products, iterate_step(): jnp.dot(poly, current, preferred_element_type=jnp.float32)  107 us
    all_gather x1, waiting for transfers between devices, on_device(): lax.all_gather(up_weight, 'fsdp', axis=0, tiled=True)  88.2 us
  transfers between devices with their start and end apart: 11, of which 8 were waited for; matrix products, arithmetic and copies ran while one was open for 9% of the time, Pallas kernels for 0%

commit v1 on v0

v1 whole, which is shorter than its diff:
```python
import functools
import math

import jax
import jax.numpy as jnp
from jax import lax
from jax.experimental import pallas as pl
from jax.experimental.pallas import tpu as pltpu
from jax.sharding import PartitionSpec as P

HEADS = 15
KV_HEADS = 5
HEAD = 64
NS_ITERS = 5


EPS = 1e-05
THETA = 100000.0
NS_A = 3.4445
NS_B = -4.775
NS_C = 2.0315
MOMENTUM = 0.95
RATE = 0.2
OUT_RATE = 6.0
GAIN_RATE = 0.002
MASKED = -1e30

MESH = pl.DeviceIdType.MESH
BF16 = jnp.bfloat16
F32 = jnp.float32
ANY = pl.BlockSpec(memory_space=pl.ANY)
VMEM = pl.BlockSpec(memory_space=pltpu.VMEM)
CLASSES = 8
WIDE = 6


def contract(left, right, left_dim, right_dim):
    return lax.dot_general(
        left, right, (((left_dim,), (right_dim,)), ((), ())), preferred_element_type=jnp.float32
    )


class Place:
    def __init__(self):
        self.parts = lax.axis_size("fsdp")
        self.extra = lax.axis_size("ctx") // CLASSES
        self.c = lax.axis_index("ctx")
        self.f = lax.axis_index("fsdp")
        self.p = lax.rem(self.c, CLASSES)
        self.core = lax.rem(self.c, 2)
        self.b1 = jnp.where(self.core == 0, 2, 4)
        self.b2 = jnp.where(self.core == 0, 4, 2)

    def peer(self, bits):
        return (self.c ^ bits, self.f)

    def along(self, j):
        return (self.c, self.f ^ j)

    def other(self, j):
        groups = self.extra
        return (lax.rem(self.c + CLASSES * j, CLASSES * groups), self.f)

    def barrier(self, bits=(1, 2, 4), line=True, others=False):
        sem = pltpu.get_barrier_semaphore()
        targets = [self.peer(b) for b in bits]
        if line:
            targets += [self.along(j) for j in range(1, self.parts)]
        if others:
            targets += [self.other(j) for j in range(1, self.extra)]
        for target in targets:
            pl.semaphore_signal(sem, inc=1, device_id=target, device_id_type=MESH)
        pl.semaphore_wait(sem, len(targets))


def remote(src, dst, send, recv, target):
    return pltpu.make_async_remote_copy(
        src_ref=src, dst_ref=dst, send_sem=send, recv_sem=recv, device_id=target, device_id_type=MESH
    )


def by_kind(cls, wide, tall):
    pl.when(cls < WIDE)(wide)
    pl.when(cls >= WIDE)(tall)


def weights_kernel(in_a, in_b, out_a, out_b, local, zs, s1, s2, sc, recv):
    at = Place()
    p, f, parts = at.p, at.f, at.parts
    at.barrier()
    copies = [
        pltpu.make_async_copy(in_a, out_a.at[:, f], local.at[0]),
        pltpu.make_async_copy(in_b, out_b.at[:, f], local.at[1]),
    ]
    for copy in copies:
        copy.start()

    def act(cls, j, g, send, target, what, first=False):
        def wide():
            dst = out_a.at[cls, g]
            src = in_a.at[cls] if first else dst
            getattr(remote(src, dst, send, recv.at[cls, j], target), what)()

        def tall():
            dst = out_b.at[cls - WIDE, g]
            src = in_b.at[cls - WIDE] if first else dst
            getattr(remote(src, dst, send, recv.at[cls, j], target), what)()

        by_kind(cls, wide, tall)

    sends = []

    def send(cls, j, g, sem, target, first=False):
        act(cls, j, g, sem, target, "start", first)
        sends.append((cls, j, g, sem, target, first))

    def arrived(cls, j):
        act(cls, j, f ^ j, zs.at[j], at.along(j), "wait_recv")

    for j in range(1, parts):
        send(p, j, f, zs.at[j], at.along(j), True)
    for j in range(1, parts):
        arrived(p, j)
        send(p, j, f ^ j, s1.at[0, j], at.peer(at.b1))
        send(p, j, f ^ j, s2.at[0, j], at.peer(at.b2))
        send(p, j, f ^ j, sc.at[0, j], at.peer(1))
    for j in range(1, parts):
        arrived(p ^ at.b1, j)
        send(p ^ at.b1, j, f ^ j, s2.at[1, j], at.peer(at.b2))
        send(p ^ at.b1, j, f ^ j, sc.at[1, j], at.peer(1))
    for slot, bits in ((2, at.b2), (3, at.b1 ^ at.b2)):
        for j in range(1, parts):
            arrived(p ^ bits, j)
            send(p ^ bits, j, f ^ j, sc.at[slot, j], at.peer(1))
    for bits in (1, 3, 5, 7):
        for j in range(1, parts):
            arrived(p ^ bits, j)
    for cls, j, g, sem, target, first in sends:
        act(cls, j, g, sem, target, "wait_send", first)
    for copy in copies:
        copy.wait()


def gather_weights(wide, tall):
    parts = lax.axis_size("fsdp")
    dma = pltpu.SemaphoreType.DMA
    return pl.pallas_call(
        weights_kernel,
        out_shape=(
            jax.ShapeDtypeStruct((WIDE, parts) + wide.shape[1:], BF16),
            jax.ShapeDtypeStruct((CLASSES - WIDE, parts) + tall.shape[1:], BF16),
        ),
        in_specs=[ANY, ANY],
        out_specs=(ANY, ANY),
        scratch_shapes=[
            dma((2,)),
            dma((parts,)),
            dma((1, parts)),
            dma((2, parts)),
            dma((4, parts)),
            dma((CLASSES, parts)),
        ],
        compiler_params=pltpu.CompilerParams(collective_id=0, has_side_effects=True),
        name="gather_weights",
    )(wide, tall)


def spread(at, own_a, own_b, out_a, out_b, local, ss, recv):
    p = at.p

    def act(cls, sem, target, what, first=False):
        def wide():
            dst = out_a.at[cls]
            getattr(remote(own_a if first else dst, dst, sem, recv.at[cls], target), what)()

        def tall():
            dst = out_b.at[cls - WIDE]
            getattr(remote(own_b if first else dst, dst, sem, recv.at[cls], target), what)()

        by_kind(cls, wide, tall)

    def keep(what):
        def wide():
            getattr(pltpu.make_async_copy(own_a, out_a.at[p], local), what)()

        def tall():
            getattr(pltpu.make_async_copy(own_b, out_b.at[p - WIDE], local), what)()

        by_kind(p, wide, tall)

    sends = []

    def send(cls, slot, target, first=False):
        act(cls, ss.at[slot], target, "start", first)
        sends.append((cls, slot, target, first))

    def arrived(cls):
        act(cls, ss.at[0], at.peer(1), "wait_recv")

    send(p, 0, at.peer(at.b1), True)
    send(p, 1, at.peer(at.b2), True)
    send(p, 2, at.peer(1), True)
    keep("start")

    def finish():
        arrived(p ^ at.b1)
        send(p ^ at.b1, 3, at.peer(at.b2))
        send(p ^ at.b1, 4, at.peer(1))
        arrived(p ^ at.b2)
        send(p ^ at.b2, 5, at.peer(1))
        arrived(p ^ at.b1 ^ at.b2)
        send(p ^ at.b1 ^ at.b2, 6, at.peer(1))
        for bits in (1, 3, 5, 7):
            arrived(p ^ bits)
        for cls, slot, target, first in sends:
            act(cls, ss.at[slot], target, "wait_send", first)
        keep("wait")

    return finish


def reduce_kernel(
    parts, extra, high,
    xt_in, dy_in, gain_in, m_qk, m_ov, m_gate, m_up, m_down,
    g_a, g_b, s_a, s_b, gain_out,
    xt, dy, p1s, p1r, p2s, p2r, own, own_t, za_s, za_r, zb_s, zb_r, ma, mb, ga, gb, sa, sb, es, er, gain_s, gain_r,
    ls, xs, xr, s1, r1, s2, r2, zs, zr, esem, ersem, msem, gs, gr, ag_l, ag_s, ag_r, ss, sr, sl,
):
    at = Place()
    p, f, core = at.p, at.f, at.core
    tokens = xt_in.shape[2]
    rows = ma.shape[0]
    half = dy.shape[2]

    def moment(what):
        for cls in range(CLASSES):
            @pl.when(p == cls)
            def _(cls=cls):
                side = cls % 2
                if cls < 2:
                    src, dst = (m_qk, m_ov)[cls], ma
                elif cls < WIDE:
                    whole = m_gate if cls < 4 else m_up
                    src, dst = whole.at[:, pl.ds(side * half, half)], ma
                else:
                    src, dst = m_down.at[pl.ds(side * high, high)], mb
                getattr(pltpu.make_async_copy(src, dst, msem), what)()

    moment("start")
    mine = [pltpu.make_async_copy(xt_in, xt.at[:, :, pl.ds(0, tokens)], ls.at[0])]
    for slot in range(4):
        mine.append(
            pltpu.make_async_copy(dy_in.at[core + 2 * slot], dy.at[slot, pl.ds(0, tokens)], ls.at[1 + slot])
        )
    mine.append(pltpu.make_async_copy(dy_in.at[8], dy.at[4, pl.ds(0, tokens)], ls.at[5]))
    for copy in mine:
        copy.start()
    at.barrier(others=True)
    pair = at.peer(1)
    theirs = [remote(xt_in, xt.at[:, :, pl.ds(tokens, tokens)], xs.at[0], xr.at[0], pair)]
    for slot in range(4):
        theirs.append(
            remote(dy_in.at[1 - core + 2 * slot], dy.at[slot, pl.ds(tokens, tokens)], xs.at[1 + slot], xr.at[1 + slot], pair)
        )
    theirs.append(remote(dy_in.at[8], dy.at[4, pl.ds(tokens, tokens)], xs.at[5], xr.at[5], pair))
    for copy in theirs:
        copy.start()

    def swap(slot, target):
        return remote(gain_s.at[slot], gain_r.at[slot], gs.at[slot], gr.at[slot], target)

    gain_s[0] = gain_in[...]
    swaps = [swap(0, pair)]
    swaps[0].start()
    for copy in mine:
        copy.wait()
    for copy in theirs:
        copy.wait()

    def term(cls, r):
        at_rows = pl.ds(pl.multiple_of(r * rows, rows), rows)
        slot = lax.div(cls, 2)
        kind = jnp.where(cls == 0, 0, jnp.where(cls == 1, 1, jnp.where(cls < WIDE, 2, 3)))
        value = jnp.dot(xt[kind, at_rows, :], dy[slot], preferred_element_type=F32)
        return value

    def with_values(cls, r, put):
        at_rows = pl.ds(pl.multiple_of(r * rows, rows), rows)

        @pl.when(cls == 1)
        def _():
            put(term(cls, r) + jnp.dot(xt[0, at_rows, :], dy[4], preferred_element_type=F32))

        @pl.when(cls != 1)
        def _():
            put(term(cls, r))

    def order(i):
        return lax.rem(f + 1 + i, parts)

    def one(slot, i):
        r = order(i)
        return remote(p1s.at[slot, r], p1r.at[slot, r], s1.at[slot, r], r1.at[slot, r], at.peer(at.b1))

    for slot, bits in ((0, at.b1 ^ at.b2), (1, at.b1)):
        def first(i, carry, slot=slot, bits=bits):
            r = order(i)

            def put(value):
                p1s[slot, r] = value.astype(BF16)

            with_values(p ^ bits, r, put)
            one(slot, i).start()
            return carry

        lax.fori_loop(0, parts, first, 0)

    swaps[0].wait()
    gain_s[1] = gain_s[0] + gain_r[0]
    swaps.append(swap(1, at.peer(2)))
    swaps[1].start()

    def two(i):
        r = order(i)
        return remote(p2s.at[r], p2r.at[r], s2.at[r], r2.at[r], at.peer(at.b2))

    def second(i, carry):
        r = order(i)
        one(0, i).wait_recv()

        def put(value):
            p2s[r] = (value + p1r[0, r].astype(F32)).astype(BF16)

        with_values(p ^ at.b2, r, put)
        two(i).start()
        return carry

    lax.fori_loop(0, parts, second, 0)
    swaps[1].wait()
    gain_s[2] = gain_s[1] + gain_r[1]
    swaps.append(swap(2, at.peer(4)))
    swaps[2].start()

    def line_a(r, source):
        return remote(za_s.at[r], za_r.at[source], zs.at[r], zr.at[source], (at.c, r))

    def line_b(r, source):
        return remote(
            zb_s.at[pl.ds(pl.multiple_of(r * high, high), high)],
            zb_r.at[source], zs.at[r], zr.at[source], (at.c, r),
        )

    early = extra == 1

    def third(i, carry):
        r = order(i)
        one(1, i).wait_recv()
        two(i).wait_recv()

        def put(value):
            total = value + p1r[1, r].astype(F32) + p2r[r].astype(F32)
            own[r] = total
            if early:
                za_s[r] = total.astype(BF16)

        with_values(p, r, put)
        if early:
            @pl.when((p < WIDE) & (i < parts - 1))
            def _():
                line_a(r, f).start()
        return carry

    lax.fori_loop(0, parts, third, 0)
    swaps[2].wait()
    gain_s[3] = gain_s[2] + gain_r[2]

    if not early:
        es[...] = own[...].astype(BF16)
        group = [
            remote(es, er.at[j - 1], esem.at[j - 1], ersem.at[j - 1], at.other(j)) for j in range(1, extra)
        ]
        for copy in group:
            copy.start()
        for j in range(1, extra):
            group[j - 1].wait_recv()
            own[...] = own[...] + er[j - 1].astype(F32)
        for copy in group:
            copy.wait_send()
        za_s[...] = own[...].astype(BF16)

        @pl.when(p < WIDE)
        def _():
            for j in range(1, parts):
                line_a(f ^ j, f).start()

    @pl.when(p >= WIDE)
    def _():
        for tile in range(half // 128):
            for r in range(parts):
                block = own[r, :, pl.ds(tile * 128, 128)]
                if rows % 128 == 0:
                    own_t[pl.ds(tile * 128, 128), pl.ds(r * rows, rows)] = block.T
            if rows % 128 != 0:
                column = own[:, :, pl.ds(tile * 128, 128)].reshape(parts * rows, 128)
                own_t[pl.ds(tile * 128, 128), :] = column.T
        zb_s[...] = own_t[...].astype(BF16)
        for j in range(1, parts):
            line_b(f ^ j, f).start()

    line_gain = [
        remote(gain_s.at[3], gain_r.at[3 + j], gs.at[3 + j], gr.at[3 + j], at.along(j)) for j in range(1, parts)
    ]
    other_gain = []
    for copy in line_gain:
        copy.start()

    moment("wait")

    @pl.when(p < WIDE)
    def _():
        total = own[f]
        for j in range(1, parts):
            line_a(f ^ j, f ^ j).wait_recv()
            total = total + za_r[f ^ j].astype(F32)
        ga[...] = total.astype(BF16)
        sa[...] = (MOMENTUM * ma[...] + total).astype(BF16)

    @pl.when(p >= WIDE)
    def _():
        total = own_t[pl.ds(pl.multiple_of(f * high, high), high), :]
        for j in range(1, parts):
            line_b(f ^ j, f ^ j).wait_recv()
            total = total + zb_r[f ^ j].astype(F32)
        gb[...] = total.astype(BF16)
        sb[...] = (MOMENTUM * mb[...] + total).astype(BF16)

    def share_a(j, source):
        return remote(sa, s_a.at[pl.ds(pl.multiple_of(source * rows, rows), rows)], ss.at[j], sr.at[j], at.along(j))

    def share_b(j, source):
        return remote(sb, s_b.at[pl.ds(pl.multiple_of(source * high, high), high)], ss.at[j], sr.at[j], at.along(j))

    @pl.when(p < WIDE)
    def _():
        for j in range(1, parts):
            share_a(j, f).start()
        pltpu.make_async_copy(sa, s_a.at[pl.ds(pl.multiple_of(f * rows, rows), rows)], sl).start()

    @pl.when(p >= WIDE)
    def _():
        for j in range(1, parts):
            share_b(j, f).start()
        pltpu.make_async_copy(sb, s_b.at[pl.ds(pl.multiple_of(f * high, high), high)], sl).start()

    finish = spread(at, ga, gb, g_a, g_b, ag_l, ag_s, ag_r)
    total = gain_s[3]
    for j in range(1, parts):
        line_gain[j - 1].wait()
        total = total + gain_r[3 + j]
    if extra > 1:
        gain_s[4] = total
        other_gain = [
            remote(gain_s.at[4], gain_r.at[3 + parts + j], gs.at[3 + parts + j], gr.at[3 + parts + j], at.other(j))
            for j in range(1, extra)
        ]
        for copy in other_gain:
            copy.start()
        for j in range(1, extra):
            other_gain[j - 1].wait()
            total = total + gain_r[3 + parts + j]
    gain_out[...] = total
    finish()

    for slot in range(2):
        lax.fori_loop(0, parts, lambda i, carry, slot=slot: (one(slot, i).wait_send(), carry)[1], 0)
    lax.fori_loop(0, parts, lambda i, carry: (two(i).wait_send(), carry)[1], 0)

    @pl.when(p < WIDE)
    def _():
        for j in range(1, parts):
            line_a(f ^ j, f).wait_send()
            share_a(j, f).wait_send()
            share_a(j, f ^ j).wait_recv()
        pltpu.make_async_copy(sa, s_a.at[pl.ds(pl.multiple_of(f * rows, rows), rows)], sl).wait()

    @pl.when(p >= WIDE)
    def _():
        for j in range(1, parts):
            line_b(f ^ j, f).wait_send()
            share_b(j, f).wait_send()
            share_b(j, f ^ j).wait_recv()
        pltpu.make_async_copy(sb, s_b.at[pl.ds(pl.multiple_of(f * high, high), high)], sl).wait()


def reduce_gradients(xt, dy, gains, moments, rows, high):
    parts = lax.axis_size("fsdp")
    extra = lax.axis_size("ctx") // CLASSES
    kinds, depth, tokens = xt.shape
    half = dy.shape[2]
    dma = pltpu.SemaphoreType.DMA
    vm = pltpu.VMEM
    n_gain = 4 + parts + extra
    group = max(extra - 1, 1)
    spare = (parts, rows, half) if extra > 1 else (1, 16, 128)
    return pl.pallas_call(
        functools.partial(reduce_kernel, parts, extra, high),
        out_shape=(
            jax.ShapeDtypeStruct((WIDE, rows, half), BF16),
            jax.ShapeDtypeStruct((CLASSES - WIDE, high, depth), BF16),
            jax.ShapeDtypeStruct((depth, half), BF16),
            jax.ShapeDtypeStruct((half, depth), BF16),
            jax.ShapeDtypeStruct(gains.shape, F32),
        ),
        in_specs=[ANY, ANY, VMEM] + [ANY] * 5,
        out_specs=(ANY, ANY, ANY, ANY, VMEM),
        scratch_shapes=[
            vm((kinds, depth, 2 * tokens), BF16),
            vm((5, 2 * tokens, half), BF16),
            vm((2, parts, rows, half), BF16),
            vm((2, parts, rows, half), BF16),
            vm((parts, rows, half), BF16),
            vm((parts, rows, half), BF16),
            vm((parts, rows, half), F32),
            vm((half, depth), F32),
            vm((parts, rows, half), BF16),
            vm((parts, rows, half), BF16),
            vm((half, depth), BF16),
            vm((parts, high, depth), BF16),
            vm((rows, half), F32),
            vm((high, depth), F32),
            vm((rows, half), BF16),
            vm((high, depth), BF16),
            vm((rows, half), BF16),
            vm((high, depth), BF16),
            vm(spare, BF16),
            vm((group,) + spare, BF16),
            vm((5,) + gains.shape, F32),
            vm((n_gain,) + gains.shape, F32),
            dma((6,)), dma((6,)), dma((6,)),
            dma((2, parts)), dma((2, parts)), dma((parts,)), dma((parts,)), dma((parts,)), dma((parts,)),
            dma((group,)), dma((group,)), dma, dma((n_gain,)), dma((n_gain,)),
            dma, dma((7,)), dma((CLASSES,)), dma((parts,)), dma((parts,)), dma,
        ],
        compiler_params=pltpu.CompilerParams(
            collective_id=1, has_side_effects=True, vmem_limit_bytes=62 << 20
        ),
        name="reduce_gradients",
    )(xt, dy, gains, *moments)


def rounded(value):
    return value.astype(BF16)


def poly_rows(g, row_start, count):
    block = g[pl.ds(row_start, count), :]
    return rounded(NS_B * block.astype(F32) + NS_C * jnp.dot(block, g[...], preferred_element_type=F32))


def ortho_kernel(
    parts, rows, high, narrow,
    s_a, s_b, o_a, o_b,
    x, x_t, gs, gr, g, poly, sq, sq_r, pa, pb, kt,
    gsem, rsem, qs, qr, ag_l, ag_s, ag_r,
):
    at = Place()
    p, f = at.p, at.f
    depth, half = x.shape
    step = depth // 4
    at.barrier(line=False)
    pair = at.peer(1)

    @pl.when(p < WIDE)
    def _():
        x[...] = s_a[...]

    @pl.when(p >= WIDE)
    def _():
        for tile in range(half // 128):
            x[:, pl.ds(tile * 128, 128)] = s_b[pl.ds(tile * 128, 128), :].T

    def scale_of(total):
        return 1.0 / (jnp.sqrt(total) + 1e-07)

    def normal(ref, inverse):
        ref[...] = rounded(ref[...].astype(F32) * inverse)

    def exchange(slot, r):
        chunk = pl.ds(r * step, step)
        return remote(gs.at[chunk], gr.at[slot, chunk], gsem.at[r], rsem.at[slot, r], pair)

    def fill_poly():
        for r in range(4):
            poly[pl.ds(r * step, step), :] = poly_rows(g, r * step, step)

    my_rows = pl.ds(pl.multiple_of(f * rows, rows), rows)
    my_high = pl.ds(pl.multiple_of(f * high, high), high)

    @pl.when(p >= 2)
    def _():
        wide = x[...].astype(F32)
        sq[...] = jnp.broadcast_to(jnp.sum(wide * wide), sq.shape)
        copy = remote(sq, sq_r, qs, qr, pair)
        copy.start()
        copy.wait()
        normal(x, scale_of(sq[...] + sq_r[...])[:1, :1])

        def grams(slot):
            for r in range(4):
                gs[pl.ds(r * step, step), :] = rounded(contract(x[pl.ds(r * step, step), :], x[...], 1, 1))
                exchange(slot, r).start()
            for r in range(4):
                chunk = pl.ds(r * step, step)
                exchange(slot, r).wait()
                g[chunk, :] = rounded(gs[chunk, :].astype(F32) + gr[slot, chunk, :].astype(F32))

        def iterate(it, carry):
            grams(lax.rem(it, 2))
            fill_poly()
            for tile in range(half // 256):
                block = pl.ds(tile * 256, 256)
                x[:, block] = rounded(
                    NS_A * x[:, block].astype(F32) + jnp.dot(poly[...], x[:, block], preferred_element_type=F32)
                )
            return carry

        lax.fori_loop(0, NS_ITERS - 1, iterate, 0)
        grams((NS_ITERS - 1) % 2)

        @pl.when(p < WIDE)
        def _():
            mine = poly_rows(g, pl.multiple_of(f * rows, rows), rows)
            pa[...] = rounded(NS_A * x[my_rows, :].astype(F32) + jnp.dot(mine, x[...], preferred_element_type=F32))

        @pl.when(p >= WIDE)
        def _():
            fill_poly()
            for tile in range(half // 128):
                x_t[pl.ds(tile * 128, 128), :] = x[:, pl.ds(tile * 128, 128)].T
            block = x_t[my_high, :]
            pb[...] = rounded(NS_A * block.astype(F32) + jnp.dot(block, poly[...], preferred_element_type=F32))

    @pl.when(p < 2)
    def _():
        kt[...] = x[:, narrow:].T
        inverse_k = scale_of(jnp.sum(jnp.square(kt[...].astype(F32))))
        normal(kt, inverse_k)
        wide = x[:, :narrow].astype(F32)
        x[:, :narrow] = rounded(wide * scale_of(jnp.sum(wide * wide)))

        def narrow_step(it, carry):
            gram = rounded(contract(kt[...], kt[...], 1, 1))
            turn = rounded(NS_B * gram.astype(F32) + NS_C * jnp.dot(gram, gram, preferred_element_type=F32))
            kt[...] = rounded(NS_A * kt[...].astype(F32) + jnp.dot(turn, kt[...], preferred_element_type=F32))
            return carry

        lax.fori_loop(0, NS_ITERS, narrow_step, 0)

        def gram_of():
            for r in range(4):
                chunk = pl.ds(r * step, step)
                g[chunk, :] = rounded(contract(x[chunk, :narrow], x[:, :narrow], 1, 1))

        def square_step(it, carry):
            gram_of()
            fill_poly()
            x[:, :narrow] = rounded(
                NS_A * x[:, :narrow].astype(F32) + jnp.dot(poly[...], x[:, :narrow], preferred_element_type=F32)
            )
            return carry

        lax.fori_loop(0, NS_ITERS - 1, square_step, 0)
        gram_of()
        mine = poly_rows(g, pl.multiple_of(f * rows, rows), rows)
        square = rounded(
            NS_A * x[my_rows, :narrow].astype(F32) + jnp.dot(mine, x[:, :narrow], preferred_element_type=F32)
        )
        x[:, narrow:] = kt[...].T
        pa[:, :narrow] = square
        pa[:, narrow:] = x[my_rows, narrow:]

    spread(at, pa, pb, o_a, o_b, ag_l, ag_s, ag_r)()


def orthogonalize(s_a, s_b, rows, high, narrow):
    parts = lax.axis_size("fsdp")
    depth, half = s_a.shape
    dma = pltpu.SemaphoreType.DMA
    vm = pltpu.VMEM
    return pl.pallas_call(
        functools.partial(ortho_kernel, parts, rows, high, narrow),
        out_shape=(
            jax.ShapeDtypeStruct((WIDE, rows, half), BF16),
            jax.ShapeDtypeStruct((CLASSES - WIDE, high, depth), BF16),
        ),
        in_specs=[VMEM, VMEM],
        out_specs=(ANY, ANY),
        scratch_shapes=[
            vm((depth, half), BF16),
            vm((half, depth), BF16),
            vm((depth, depth), BF16),
            vm((2, depth, depth), BF16),
            vm((depth, depth), BF16),
            vm((depth, depth), BF16),
            vm((8, 128), F32),
            vm((8, 128), F32),
            vm((rows, half), BF16),
            vm((high, depth), BF16),
            vm((half - narrow, depth), BF16),
            dma((4,)), dma((2, 4)), dma, dma, dma, dma((7,)), dma((CLASSES,)),
        ],
        compiler_params=pltpu.CompilerParams(
            collective_id=2, has_side_effects=True, vmem_limit_bytes=62 << 20
        ),
        name="orthogonalize",
    )(s_a, s_b)


def rotary_tables(positions, width):
    half = width // 2
    frequency = THETA ** (-(jnp.arange(half, dtype=jnp.float32) * 2.0 / width))
    angle = positions.astype(jnp.float32)[:, None] * frequency[None, :]
    return (jnp.cos(angle)[:, None, :], jnp.sin(angle)[:, None, :])


def rotate(value, cosine, sine):
    half = value.shape[-1] // 2
    first = value[..., :half]
    second = value[..., half:]
    return jnp.concatenate(
        [first * cosine - second * sine, second * cosine + first * sine], axis=-1
    )


def unrotate(incoming, cosine, sine):
    half = incoming.shape[-1] // 2
    upper = incoming[..., :half]
    lower = incoming[..., half:]
    return jnp.concatenate([upper * cosine + lower * sine, lower * cosine - upper * sine], axis=-1)


def norm_forward(residual, gain):
    inverse = lax.rsqrt(jnp.mean(residual * residual, axis=-1, keepdims=True) + EPS)
    return ((residual * inverse * gain).astype(jnp.bfloat16), inverse)


def norm_backward(residual, inverse, gain, incoming):
    scaled = incoming * gain
    through = inverse * scaled - residual * inverse**3 * jnp.mean(
        scaled * residual, axis=-1, keepdims=True
    )
    return (through, jnp.sum(incoming * residual * inverse, axis=0))


def padded(array, axis, parts, count, full):
    if count == full:
        return array
    shape = array.shape
    split = array.reshape(shape[:axis] + (parts, count) + shape[axis + 1 :])
    pads = [(0, 0)] * split.ndim
    pads[axis + 1] = (0, full - count)
    return jnp.pad(split, pads).reshape(shape[:axis] + (parts * full,) + shape[axis + 1 :])


def trimmed(array, axis, parts, count, full):
    if count == full:
        return array
    shape = array.shape
    split = array.reshape(shape[:axis] + (parts, full) + shape[axis + 1 :])
    kept = lax.slice_in_dim(split, 0, count, axis=axis + 1)
    return kept.reshape(shape[:axis] + (parts * count,) + shape[axis + 1 :])


def on_device(
    layer_input,
    output_grad,
    query_weight,
    key_weight,
    value_weight,
    output_weight,
    gate_weight,
    up_weight,
    down_weight,
    norm_gains,
    query_momentum,
    key_momentum,
    value_momentum,
    output_momentum,
    gate_momentum,
    up_momentum,
    down_momentum,
    gain_momentum,
    block_order,
):
    rows = layer_input.shape[1]
    block = rows // 2
    group = HEADS // KV_HEADS
    scale = 1.0 / math.sqrt(HEAD)
    parts = lax.axis_size("fsdp")
    ctx_place = lax.axis_index("ctx")
    width = layer_input.shape[2]
    hidden_size = gate_weight.shape[1]
    half = hidden_size // 2
    kv = key_weight.shape[1]
    short = width // parts
    full = -(-short // 16) * 16
    high = half // parts
    offsets = jnp.arange(block, dtype=jnp.int32)
    own_blocks = lax.dynamic_slice_in_dim(block_order, 2 * ctx_place, 2)
    query_pos = (own_blocks[:, None] * block + offsets[None, :]).reshape(rows)
    key_pos = (block_order[:, None] * block + offsets[None, :]).reshape(-1)

    wide = jnp.stack(
        [
            jnp.concatenate([query_weight, key_weight], axis=1),
            jnp.concatenate([output_weight, value_weight], axis=1),
            gate_weight[:, :half],
            gate_weight[:, half:],
            up_weight[:, :half],
            up_weight[:, half:],
        ]
    )
    all_wide, all_tall = gather_weights(wide, down_weight.reshape(2, high, width))
    w_qk, w_ov, w_gate_0, w_gate_1, w_up_0, w_up_1 = [all_wide[i].reshape(width, half) for i in range(WIDE)]
    w_down = [all_tall[i].reshape(half, width) for i in range(2)]

    residual = layer_input[0].astype(jnp.float32)
    normed_first, inverse_first = norm_forward(residual, norm_gains[0])
    qk_pre = jnp.dot(normed_first, w_qk, preferred_element_type=jnp.float32)
    query_pre = qk_pre[:, :width].reshape(rows, HEADS, HEAD)
    key_pre = qk_pre[:, width:].reshape(rows, KV_HEADS, HEAD)
    value_low = (
        jnp.dot(normed_first, w_ov, preferred_element_type=jnp.float32)[:, width:]
        .astype(jnp.bfloat16)
        .reshape(rows, KV_HEADS, HEAD)
    )
    cosine, sine = rotary_tables(query_pos, HEAD)
    query_rot = rotate(query_pre, cosine, sine).astype(jnp.bfloat16)
    key_rot = rotate(key_pre, cosine, sine).astype(jnp.bfloat16)
    keys_all, values_all = (
        lax.all_gather(key_rot, "ctx", axis=0, tiled=True),
        lax.all_gather(value_low, "ctx", axis=0, tiled=True),
    )
    keys_head = keys_all.transpose(1, 0, 2)
    values_head = values_all.transpose(1, 0, 2)
    queries_head = (
        query_rot.reshape(rows, KV_HEADS, group, HEAD)
        .transpose(1, 2, 0, 3)
        .reshape(KV_HEADS, group * rows, HEAD)
    )
    row_pos = jnp.tile(query_pos, group)
    allowed = key_pos[None, :] <= row_pos[:, None]

    def head_forward(item):
        query, key, value = item
        scores = jnp.where(allowed, contract(query, key, 1, 1) * scale, MASKED)
        top = jnp.max(scores, axis=-1, keepdims=True)
        expo = jnp.exp(scores - top)
        total = jnp.sum(expo, axis=-1, keepdims=True)
        probs_low = (expo / total).astype(jnp.bfloat16)
        return (
            jnp.dot(probs_low, value, preferred_element_type=jnp.float32),
            (top + jnp.log(total))[:, 0],
        )

    mixed, log_total = lax.map(head_forward, (queries_head, keys_head, values_head))
    attended = (
        mixed.reshape(KV_HEADS, group, rows, HEAD)
        .transpose(2, 0, 1, 3)
        .reshape(rows, HEADS * HEAD)
        .astype(jnp.bfloat16)
    )
    w_out = w_ov[:, :width]
    middle = residual + jnp.dot(attended, w_out, preferred_element_type=jnp.float32)
    normed_second, inverse_second = norm_forward(middle, norm_gains[1])

    def sides(left, right):
        return jnp.concatenate([left, right], axis=1)

    gate = sides(
        jnp.dot(normed_second, w_gate_0, preferred_element_type=jnp.float32),
        jnp.dot(normed_second, w_gate_1, preferred_element_type=jnp.float32),
    )
    lifted = sides(
        jnp.dot(normed_second, w_up_0, preferred_element_type=jnp.float32),
        jnp.dot(normed_second, w_up_1, preferred_element_type=jnp.float32),
    )
    sigma = jax.nn.sigmoid(gate)
    hidden = (gate * sigma * lifted).astype(jnp.bfloat16)
    hidden_split = hidden.reshape(rows, parts, 2, high)
    hidden_sides = [hidden_split[:, :, i].reshape(rows, half) for i in range(2)]
    layer_output = (
        middle
        + jnp.dot(hidden_sides[0], w_down[0], preferred_element_type=jnp.float32)
        + jnp.dot(hidden_sides[1], w_down[1], preferred_element_type=jnp.float32)
    ).astype(jnp.bfloat16)
    upstream = output_grad[0]
    grad_hidden = jnp.stack(
        [contract(upstream, w_down[i], 1, 1).reshape(rows, parts, high) for i in range(2)], axis=2
    ).reshape(rows, hidden_size)
    grad_gate = (grad_hidden * lifted * sigma * (1.0 + gate * (1.0 - sigma))).astype(jnp.bfloat16)
    grad_lifted = (grad_hidden * gate * sigma).astype(jnp.bfloat16)
    grad_normed_second = (
        contract(grad_gate[:, :half], w_gate_0, 1, 1)
        + contract(grad_gate[:, half:], w_gate_1, 1, 1)
        + contract(grad_lifted[:, :half], w_up_0, 1, 1)
        + contract(grad_lifted[:, half:], w_up_1, 1, 1)
    )
    through_second, gain_second = norm_backward(
        middle, inverse_second, norm_gains[1], grad_normed_second
    )
    grad_middle = upstream.astype(jnp.float32) + through_second
    grad_branch = grad_middle.astype(jnp.bfloat16)
    grad_attended = contract(grad_branch, w_out, 1, 1).astype(jnp.bfloat16)
    grad_heads = (
        grad_attended.reshape(rows, KV_HEADS, group, HEAD)
        .transpose(1, 2, 0, 3)
        .reshape(KV_HEADS, group * rows, HEAD)
    )

    def head_backward(item):
        query, key, value, grad_out, log_row = item
        scores = jnp.where(allowed, contract(query, key, 1, 1) * scale, MASKED)
        probs = jnp.exp(scores - log_row[:, None])
        grad_value_part = contract(probs.astype(jnp.bfloat16), grad_out, 0, 0)
        grad_probs = contract(grad_out, value, 1, 1)
        grad_scores = (
            probs * (grad_probs - jnp.sum(grad_probs * probs, axis=-1, keepdims=True))
        ).astype(jnp.bfloat16)
        grad_query_part = jnp.dot(grad_scores, key, preferred_element_type=jnp.float32) * scale
        grad_key_part = contract(grad_scores, query, 0, 0) * scale
        return (grad_query_part, grad_key_part, grad_value_part)

    grad_query_rot, grad_key_all, grad_value_all = lax.map(
        head_backward, (queries_head, keys_head, values_head, grad_heads, log_total)
    )
    grad_key_own, grad_value_own = (
        lax.psum_scatter(
            grad_key_all.astype(jnp.bfloat16), "ctx", scatter_dimension=1, tiled=True
        ).astype(jnp.float32),
        lax.psum_scatter(
            grad_value_all.astype(jnp.bfloat16), "ctx", scatter_dimension=1, tiled=True
        ).astype(jnp.float32),
    )
    grad_query = (
        unrotate(
            grad_query_rot.reshape(KV_HEADS, group, rows, HEAD)
            .transpose(2, 0, 1, 3)
            .reshape(rows, HEADS, HEAD),
            cosine,
            sine,
        )
        .reshape(rows, HEADS * HEAD)
        .astype(jnp.bfloat16)
    )
    grad_key = (
        unrotate(grad_key_own.transpose(1, 0, 2), cosine, sine)
        .reshape(rows, KV_HEADS * HEAD)
        .astype(jnp.bfloat16)
    )
    grad_value = (
        grad_value_own.transpose(1, 0, 2).reshape(rows, KV_HEADS * HEAD).astype(jnp.bfloat16)
    )
    grad_qk = sides(grad_query, grad_key)
    zero_query = jnp.zeros((rows, width), jnp.bfloat16)
    grad_v = sides(zero_query, grad_value)
    grad_normed_first = contract(grad_qk, w_qk, 1, 1) + contract(grad_v, w_ov, 1, 1)
    through_first, gain_first = norm_backward(
        residual, inverse_first, norm_gains[0], grad_normed_first
    )
    input_gradient = (grad_middle + through_first)[None]

    xt = jnp.stack([item.T for item in (normed_first, attended, normed_second, upstream)])
    xt = padded(xt, 1, parts, short, full)
    dy = jnp.stack(
        [
            grad_qk,
            sides(grad_branch, jnp.zeros((rows, kv), jnp.bfloat16)),
            grad_gate[:, :half],
            grad_gate[:, half:],
            grad_lifted[:, :half],
            grad_lifted[:, half:],
            hidden_sides[0],
            hidden_sides[1],
            grad_v,
        ]
    )
    gains = jnp.pad(jnp.stack([gain_first, gain_second]), ((0, 6), (0, 0)))

    def pad_rows(array):
        return padded(array, 0, 1, short, full)

    def pad_columns(array):
        return padded(array, 1, parts, short, full)

    moments = (
        pad_rows(sides(query_momentum, key_momentum)),
        pad_rows(sides(output_momentum, value_momentum)),
        pad_rows(gate_momentum),
        pad_rows(up_momentum),
        pad_columns(down_momentum),
    )
    g_wide, g_tall, s_wide, s_tall, gain_sum = reduce_gradients(xt, dy, gains, moments, full, high)
    o_wide, o_tall = orthogonalize(s_wide, s_tall, full, high, width)

    def unpack(wide_pieces, tall_pieces):
        pieces = wide_pieces[:, :short]
        tall = trimmed(tall_pieces, 2, parts, short, full).reshape(2 * high, width)
        return (
            pieces[0, :, :width],
            pieces[0, :, width:],
            pieces[1, :, width:],
            pieces[1, :, :width],
            sides(pieces[2], pieces[3]),
            sides(pieces[4], pieces[5]),
            tall,
        )

    gradients = [item.astype(jnp.float32) for item in unpack(g_wide, g_tall)]
    orthos = unpack(o_wide, o_tall)
    olds = (
        query_momentum,
        key_momentum,
        value_momentum,
        output_momentum,
        gate_momentum,
        up_momentum,
        down_momentum,
    )
    moments = [MOMENTUM * old + new for old, new in zip(olds, gradients)]
    old_weights = (
        query_weight,
        key_weight,
        value_weight,
        output_weight,
        gate_weight,
        up_weight,
        down_weight,
    )
    new_weights = []
    for index in range(len(olds)):
        cols_full = old_weights[index].shape[1]
        rows_full = old_weights[index].shape[0] * parts
        step_rate = OUT_RATE if index == 3 else RATE
        factor = -step_rate * max(1.0, cols_full / rows_full) ** 0.5
        new_weights.append(
            old_weights[index].astype(jnp.float32) + factor * orthos[index].astype(jnp.float32)
        )
    gain_width = norm_gains.shape[1] // parts
    place = lax.axis_index("fsdp") * gain_width
    gain_gradient = lax.dynamic_slice_in_dim(gain_sum[:2], place, gain_width, 1)
    gain_shard = lax.dynamic_slice_in_dim(norm_gains, place, gain_width, 1)
    gain_moment = MOMENTUM * gain_momentum + gain_gradient
    new_gains = gain_shard - GAIN_RATE * gain_moment
    return (
        layer_output[None],
        input_gradient,
        *gradients,
        gain_gradient,
        *moments,
        gain_moment,
        *new_weights,
        new_gains,
    )


def solution(mesh):
    tokens = P("fsdp", "ctx", None)
    shard = P("fsdp", None)
    gains = P(None, "fsdp")
    return jax.shard_map(
        on_device,
        mesh=mesh,
        in_specs=(tokens, tokens) + (shard,) * 7 + (P(),) + (shard,) * 7 + (gains, P()),
        out_specs=(tokens, tokens) + ((shard,) * 7 + (gains,)) * 3,
        check_vma=False,
    )
```

time: 2580 us -> 784 us (0.30)
  waiting for transfers between devices: 1220 us -> 25.9 us
  local copies, waits for them, and re-layouts: 686 us -> 113 us
  Pallas kernels: 0 us -> 455 us
  matrix products: 290 us -> 80.1 us
  other arithmetic: 232 us -> 57.2 us
  blocking collectives: 72.5 us -> 23.7 us
  loops' own time: 36.2 us -> 0.36 us
    unnamed x13 -> x4, waiting for transfers between devices: 731 us -> 25.9 us
    pallas_call x0 -> x3, Pallas kernels: none -> 455 us  [the longest x1 187 us: reduce_gradients(): pl.pallas_call(functools.partial(reduce_kernel, parts, extra, high), out_...]
    all_gather x5 -> x0, waiting for transfers between devices: 257 us -> none  [the longest x1 88.2 us: on_device(): lax.all_gather(up_weight, 'fsdp', axis=0, tiled=True)]
    all_to_all x2 -> x0, waiting for transfers between devices: 234 us -> none  [the longest x1 126 us: on_device(): lax.all_to_all(outgoing, 'fsdp', split_axis=0, concat_axis=0, tiled=True)]
    reshape x36 -> x2, local copies, waits for them, and re-layouts: 233 us -> 2.94 us  [the longest x1 2.78 us: on_device(): grad_hidden = jnp.stack([contract(upstream, w_down[i], 1, 1).reshape(rows...]
    unnamed x184 -> x193, local copies, waits for them, and re-layouts: 284 us -> 55.9 us
    dot_general x17 -> x9, matrix products: 124 us -> 10.5 us  [the longest x1 2.25 us: on_device(): qk_pre = jnp.dot(normed_first, w_qk, preferred_element_type=jnp.float32)]
    dot_general x49 -> x34, matrix products: 152 us -> 52.4 us  [contract(): lax.dot_general(left, right, (((left_dim,), (right_dim,)), ((), ())), pre...]
  transfers between devices with their start and end apart: 11 -> 2, of which waited for: 8 -> 1; matrix products, arithmetic and copies ran while one was open for 9% -> 6% of each run, Pallas kernels for 0% -> 0%
where the time goes in v1:
time: 784 us; the launch traced here: 771 us
  Pallas kernels  455 us (58%)
  local copies, waits for them, and re-layouts  113 us (14%)
  matrix products  80.1 us (10%)
  other arithmetic  57.2 us (7%)
  waiting for transfers between devices  25.9 us (3%)
  blocking collectives  23.7 us (3%)
  between operations  15.3 us (2%)
    pallas_call x1, Pallas kernels, reduce_gradients(): pl.pallas_call(functools.partial(reduce_kernel, parts, extra, high), out_...  187 us
    pallas_call x1, Pallas kernels, gather_weights(): pl.pallas_call(weights_kernel, out_shape=(jax.ShapeDtypeStruct((WIDE, par...  158 us
    pallas_call x1, Pallas kernels, orthogonalize(): pl.pallas_call(functools.partial(ortho_kernel, parts, rows, high, narrow)...  110 us
    unnamed x193, local copies, waits for them, and re-layouts  55.9 us
    dot_general x34, matrix products, contract(): lax.dot_general(left, right, (((left_dim,), (right_dim,)), ((), ())), pre...  52.4 us
    unnamed x4, waiting for transfers between devices  25.9 us
  transfers between devices with their start and end apart: 2, of which 1 were waited for; matrix products, arithmetic and copies ran while one was open for 6% of the time, Pallas kernels for 0%

profile of v1, /device:TPU:0, one launch (start us, length us, event | category | flops | bytes accessed | tf_op | source)
XLA Modules:
  0.0 771.0 jit_solution(4867698212704029081)
XLA Ops:
  18.7 158.1 %gather_weights.1 = (bf16[6,4,240,1280]{3,2,1,0:T(8,128)(2,1)}, bf16[2,4,320,960]{3,2,1,0:T(8,128)(2,1)}) custom-call(bf16[6,240,1280]{2,1,0:T(8,128)(2,1)} %bitcast_dynamic-update-slice_fusion.in_a, bf16[2,320,960]{2,1,0:T(8,128)(2,1)} %bitcast.363), custom_call_target="tpu_custom_call" | custom-call | tf_op jit(solution)/shard_map/gather_weights/pallas_call | solution.py:147
  176.8 10.2 %fusion.98 = (bf16[1,4,240,1280]{3,2,1,0:T(8,128)(2,1)}, bf16[1,4,240,1280]{3,2,1,0:T(8,128)(2,1)}, bf16[1,4,240,1280]{3,2,1,0:T(8,128)(2,1)}, bf16[1,4,240,1280...) fusion(bf16[6,4,240,1280]{3,2,1,0:T(8,128)(2,1)} %get-tuple-element.127), kind=kLoop, calls=%fused_computation.204 | loop fusion | bytes 29491200 | tf_op jit(solution)/shard_map/slice | solution.py:824
  194.1 10.3 %all_gather.6 = bf16[1024,5,64]{0,2,1:T(8,128)(2,1)S(1)} all-gather(bf16[128,5,64]{0,2,1:T(8,128)(2,1)S(1)} %pad_maximum_fusion.9), channel_id=1, replica_groups=mesh['ctx'=8,'fsdp'=4] {'ctx'}, dimensions={0}, use_global_device_ids=true | all-gather | bytes 737280 | tf_op jit(solution)/shard_map/all_gather | solution.py:841
  207.1 13.4 %all_gather.7 = bf16[1024,5,64]{2,0,1:T(8,128)(2,1)} all-gather(bf16[128,5,64]{2,0,1:T(8,128)(2,1)S(1)} %copy.218), channel_id=1, replica_groups=mesh['ctx'=8,'fsdp'=4] {'ctx'}, dimensions={0}, use_global_device_ids=true | all-gather | bytes 737280 | tf_op jit(solution)/shard_map/all_gather | solution.py:842
  220.6 23.6 %while.30 = (s32[]{:T(128)}, bf16[5,384,64]{1,2,0:T(8,128)(2,1)S(1)}, f32[5,384]{1,0:T(8,128)}, bf16[5,384,64]{2,1,0:T(8,128)(2,1)}, bf16[5,1024,64]{2,1,0:T(8,1...) while((s32[]{:T(128)}, ...), condition=%wide.region_4.5_spmd.clone.clone, body=%wide.region_1.4_spmd.clone.sunk.clone | while | flops 104201856 | bytes 5466721 | solution.py:866
  252.3 5.5 fusion.99
  263.6 2.8 copy.232
  266.4 2.8 multiply_convert_fusion.1
  278.7 47.9 %while.31 = (s32[]{:T(128)}, f32[5,384,64]{1,2,0:T(8,128)}, bf16[5,1024,64]{1,2,0:T(8,128)(2,1)}, bf16[5,1024,64]{1,2,0:T(8,128)(2,1)}, bf16[5,384,64]{2,1,0:T(8...) while((s32[]{:T(128)}, f32[5,384,64]{1,2,0:T(8,128)}, ...), condition=%wide.region_9.10_spmd.clone.clone, body=%wide.region_7.9_spmd.clone.sunk.clone | while | flops 255680128 | bytes 13617273 | solution.py:934
  326.6 3.4 copy.278
  330.0 3.9 reshape.336
  333.9 3.4 copy.280
  337.3 3.7 reshape.338
  367.2 3.4 copy.253.m_down
  370.6 3.3 pad_maximum_fusion.3
  379.9 25.9 %reduce-scatter.9.cloned.1.call-done = bf16[128,320]{1,0:T(8,128)(2,1)} async-done(((bf16[1024,320]{1,0:T(8,128)(2,1)}), bf16[128,320]{1,0:T(8,128)(2,1)}) %reduce-scatter.9.cloned.1.call-update) | async-done | bytes 81936
  419.1 186.9 %reduce_gradients.1 = (bf16[6,240,1280]{2,1,0:T(8,128)(2,1)}, bf16[2,320,960]{2,1,0:T(8,128)(2,1)}, bf16[960,1280]{1,0:T(8,128)(2,1)}, bf16[1280,960]{1,0:T(8,128)(2,1)}, f32[8,960]{1,0:T(8,128)}) custom-call(bf16[4,960,128]{2,1,0:T(8,128)(2,1)} %copy.252.xt_in, bf16[9,128,1280]{2,1,0:T(8,128)(2,1)} %fusion.77.dy_in, f32[8,960]{1,0:T(8,128)} %select_maximum_fusion.gain_in, ...), custom_call_target="tpu_custom_call" | custom-call | tf_op jit(solution)/shard_map/reduce_gradients/pallas_call | solution.py:505
  606.1 3.5 multiply_add_fusion.5
  613.2 110.0 %orthogonalize.1 = (bf16[6,240,1280]{2,1,0:T(8,128)(2,1)}, bf16[2,320,960]{2,1,0:T(8,128)(2,1)}) custom-call(bf16[960,1280]{1,0:T(8,128)(2,1)} %get-tuple-element.137.s_a, bf16[1280,960]{1,0:T(8,128)(2,1)} %get-tuple-element.138.s_b), custom_call_target="tpu_custom_call" | custom-call | tf_op jit(solution)/shard_map/orthogonalize/pallas_call | solution.py:690
  723.2 3.0 bitcast_add_fusion
  739.4 4.2 multiply_add_fusion.2
  749.1 3.8 convert_add_fusion
  753.0 2.9 multiply_add_fusion.4
  756.0 2.9 multiply_add_fusion.3
  (354 shorter events, 188.1 us)
Async XLA Ops:
  7.2 5.1 copy-start.49
  7.2 6.1 copy-start.18
  7.2 366.6 %reduce-scatter.7.cloned.1.call-start = ((), (), s32[]{:S(2)}) async-start(), calls=%async_computation.2 | async-start | bytes 884736
  10.2 4.8 copy-start.20
  176.8 10.2 %copy-start.66 = (bf16[1,128,960]{1,2,0:T(8,128)(2,1)S(1)}, bf16[1,128,960]{1,2,0:T(8,128)(2,1)}, u32[]{:S(2)}) copy-start(bf16[1,128,960]{1,2,0:T(8,128)(2,1)} %param.23) | copy-start | bytes 737284
  176.8 10.4 %copy-start.67 = (f32[2,960]{1,0:T(2,128)S(1)}, f32[2,960]{1,0:T(2,128)}, u32[]{:S(2)}) copy-start(f32[2,960]{1,0:T(2,128)} %param.32) | copy-start | bytes 23044
  187.9 17.9 %copy-start.68 = (f32[128]{0:T(128)}, f32[128]{0:T(128)S(1)}, u32[]{:S(2)}) copy-start(f32[128]{0:T(128)S(1)} %get-tuple-element.471) | copy-start | bytes 1540
  205.7 14.9 %copy-start.65 = (bf16[5,384,64]{1,2,0:T(8,128)(2,1)S(1)}, bf16[5,384,64]{1,2,0:T(8,128)(2,1)}, u32[]{:S(2)}) copy-start(bf16[5,384,64]{1,2,0:T(8,128)(2,1)} %broadcast_convert_fusion) | copy-start | bytes 737284
  258.8 16.4 %copy-start.41 = (bf16[1,128,960]{2,1,0:T(8,128)(2,1)}, bf16[1,128,960]{2,1,0:T(8,128)(2,1)S(1)}, u32[]{:S(2)}) copy-start(bf16[1,128,960]{2,1,0:T(8,128)(2,1)S(1)} %copy.229) | copy-start | bytes 737284
  269.2 4.8 copy-start.13
  333.9 71.9 %reduce-scatter.9.cloned.1.call-start = ((), (), s32[]{:S(2)}) async-start(), calls=%async_computation.3 | async-start | bytes 884736
  343.2 7.3 copy-start.44
  356.2 6.7 copy-start.33
  357.1 6.7 copy-start.31
  375.3 33.3 %copy-start.69 = (f32[128]{0:T(128)S(1)}, f32[128]{0:T(128)}, u32[]{:S(2)}) copy-start(f32[128]{0:T(128)} %copy-done.68) | copy-start | bytes 1540
  379.9 29.9 %copy-start.75 = (f32[128]{0:T(128)S(1)}, f32[128]{0:T(128)}, u32[]{:S(2)}) copy-start(f32[128]{0:T(128)} %get-tuple-element.470) | copy-start | bytes 1540
  411.0 5.1 copy-start.60
  411.1 5.8 copy-start.59
  419.1 186.9 %copy-start.24 = (f32[240,960]{1,0:T(8,128)S(1)}, f32[240,960]{1,0:T(8,128)}, u32[]{:S(2)}) copy-start(f32[240,960]{1,0:T(8,128)} %param.36) | copy-start | bytes 2764804
  419.1 186.9 %copy-start.25 = (f32[240,960]{1,0:T(8,128)S(1)}, f32[240,960]{1,0:T(8,128)}, u32[]{:S(2)}) copy-start(f32[240,960]{1,0:T(8,128)} %param.33) | copy-start | bytes 2764804
  613.2 110.0 %copy-start.48 = (bf16[240,960]{1,0:T(8,128)(2,1)S(1)}, bf16[240,960]{1,0:T(8,128)(2,1)}, u32[]{:S(2)}) copy-start(bf16[240,960]{1,0:T(8,128)(2,1)} %param.25) | copy-start | bytes 1382404
  613.2 110.1 %copy-start.50 = (bf16[240,960]{1,0:T(8,128)(2,1)S(1)}, bf16[240,960]{1,0:T(8,128)(2,1)}, u32[]{:S(2)}) copy-start(bf16[240,960]{1,0:T(8,128)(2,1)} %param.28) | copy-start | bytes 1382404
  613.2 113.0 %copy-start.54 = (bf16[240,320]{1,0:T(8,128)(2,1)S(1)}, bf16[240,320]{1,0:T(8,128)(2,1)}, u32[]{:S(2)}) copy-start(bf16[240,320]{1,0:T(8,128)(2,1)} %copy-done.53) | copy-start | bytes 460804
  739.4 5.1 copy-start.57
  (56 other events, 136.2 us)
Sparse Core Ops, SparseCore 0:
  334.0 32.9 reduce-scatter.6
  370.7 34.9 reduce-scatter.8

commit v2 on v1

--- a/solution.py
+++ b/solution.py
@@ -716,6 +716,353 @@
     )(s_a, s_b)
 
 
+class Weights:
+    def __init__(self, at, in_a, in_b, wa, wb, local, zs, s1, s2, sc, recv):
+        self.at, self.in_a, self.in_b, self.wa, self.wb = at, in_a, in_b, wa, wb
+        self.local, self.zs, self.s1, self.s2, self.sc, self.recv = local, zs, s1, s2, sc, recv
+        self.rows = in_a.shape[1]
+        self.high = in_b.shape[1]
+        self.unit = -(-self.rows // (16 * CLASSES)) * 16
+        self.last = self.rows - (CLASSES - 1) * self.unit
+        self.tall = 2 * self.high // CLASSES
+        self.sends = []
+
+    def act(self, group, q, j, plane, send, target, what, first=False):
+        recv = self.recv.at[group, q, j]
+        if group == 3:
+            side, start = lax.div(q, CLASSES // 2), lax.rem(q, CLASSES // 2) * self.tall
+            dst = self.wb.at[side, pl.ds(pl.multiple_of(plane * self.high + start, 16), self.tall)]
+            src = self.in_b.at[side, pl.ds(pl.multiple_of(start, 16), self.tall)] if first else dst
+            getattr(remote(src, dst, send, recv, target), what)()
+            return
+
+        def piece(count):
+            def go():
+                pair = pl.ds(2 * group, 2)
+                dst = self.wa.at[pair, pl.ds(pl.multiple_of(plane * self.rows + q * self.unit, 16), count)]
+                src = self.in_a.at[pair, pl.ds(pl.multiple_of(q * self.unit, 16), count)] if first else dst
+                getattr(remote(src, dst, send, recv, target), what)()
+
+            return go
+
+        pl.when(q < CLASSES - 1)(piece(self.unit))
+        pl.when(q == CLASSES - 1)(piece(self.last))
+
+    def send(self, group, q, j, plane, sem, target, first=False):
+        self.act(group, q, j, plane, sem, target, "start", first)
+        self.sends.append((group, q, j, plane, sem, target, "wait_send", first))
+
+    def arrived(self, group, q, j):
+        at = self.at
+        self.act(group, q, j, at.f ^ j, self.zs.at[group, j], at.peer(1), "wait_recv")
+
+    def keep(self):
+        f = self.at.f
+        return [
+            pltpu.make_async_copy(
+                self.in_a, self.wa.at[:, pl.ds(pl.multiple_of(f * self.rows, 16), self.rows)], self.local.at[0]
+            ),
+            pltpu.make_async_copy(
+                self.in_b, self.wb.at[:, pl.ds(pl.multiple_of(f * self.high, 16), self.high)], self.local.at[1]
+            ),
+        ]
+
+    def along(self, group):
+        at = self.at
+        for j in range(1, at.parts):
+            self.send(group, at.p, j, at.f, self.zs.at[group, j], at.along(j), True)
+
+    def first(self, group):
+        at = self.at
+        for j in range(1, at.parts):
+            self.arrived(group, at.p, j)
+            self.send(group, at.p, j, at.f ^ j, self.s1.at[group, j], at.peer(at.b1))
+            self.send(group, at.p, j, at.f ^ j, self.s2.at[group, 0, j], at.peer(at.b2))
+            self.send(group, at.p, j, at.f ^ j, self.sc.at[group, 0, j], at.peer(1))
+
+    def second(self, group):
+        at = self.at
+        q = at.p ^ at.b1
+        for j in range(1, at.parts):
+            self.arrived(group, q, j)
+            self.send(group, q, j, at.f ^ j, self.s2.at[group, 1, j], at.peer(at.b2))
+            self.send(group, q, j, at.f ^ j, self.sc.at[group, 1, j], at.peer(1))
+
+    def third(self, group):
+        at = self.at
+        for slot, bits in ((2, at.b2), (3, at.b1 ^ at.b2)):
+            for j in range(1, at.parts):
+                self.arrived(group, at.p ^ bits, j)
+                self.send(group, at.p ^ bits, j, at.f ^ j, self.sc.at[group, slot, j], at.peer(1))
+
+    def ready(self, group):
+        at = self.at
+        for bits in (1, 3, 5, 7):
+            for j in range(1, at.parts):
+                self.arrived(group, at.p ^ bits, j)
+
+    def finish(self):
+        for item in self.sends:
+            self.act(*item)
+
+
+def layer_kernel(
+    x_ref, up_ref, gains_ref, cos_ref, low_ref, high_ref, bias_ref, in_a, in_b,
+    out_ref, grad_ref, xt_ref, dy_ref, gain_ref,
+    wa, wb, probs, kv, rot, dkv, c4s, c4r, c2s, c2r, c1s, c1r, att, gate, lifted,
+    local, zs, s1, s2, sc, recv, kvs, kvr, ds, dr,
+):
+    at = Place()
+    p = at.p
+    tokens, width = x_ref.shape
+    half = wa.shape[2]
+    keys = half - width
+    group = HEADS // KV_HEADS
+    scale = 1.0 / math.sqrt(HEAD)
+    parts = at.parts
+    high = half // parts
+    wide_heads = group * tokens
+
+    weights = Weights(at, in_a, in_b, wa, wb, local, zs, s1, s2, sc, recv)
+    own = weights.keep()
+    for copy in own:
+        copy.start()
+    at.barrier()
+    for index in range(4):
+        weights.along(index)
+
+    residual = x_ref[...].astype(F32)
+    inverse_first = lax.rsqrt(jnp.mean(residual * residual, axis=-1, keepdims=True) + EPS)
+    normed_first = (residual * inverse_first * gains_ref[0:1, :]).astype(BF16)
+    xt_ref[0] = normed_first.T
+    xt_ref[3] = up_ref[...].T
+
+    weights.first(0)
+    weights.second(0)
+    weights.first(1)
+    weights.third(0)
+    for copy in own:
+        copy.wait()
+    weights.ready(0)
+
+    def turn(value, sign):
+        tiles = []
+        for tile in range(half // 128):
+            part = value[:, tile * 128 : (tile + 1) * 128]
+            swapped = pltpu.roll(part, HEAD // 2, 1) * low_ref[...] + pltpu.roll(part, 128 - HEAD // 2, 1) * high_ref[...]
+            tiles.append(part * cos_ref[...] + swapped if sign > 0 else part * cos_ref[...] - swapped)
+        return tiles
+
+    qk = jnp.dot(normed_first, wa[0], preferred_element_type=F32)
+    for tile, value in enumerate(turn(qk, 1)):
+        rot[:, tile * 128 : (tile + 1) * 128] = value.astype(BF16)
+    values = jnp.dot(normed_first, wa[1, :, width:], preferred_element_type=F32).astype(BF16)
+    kv[p, :, :keys] = rot[:, width:]
+    kv[p, :, keys:] = values
+
+    def block(q, slot, target):
+        return remote(kv.at[q], kv.at[q], kvs.at[slot], kvr.at[q], target)
+
+    sent = [block(p, 0, at.peer(at.b1)), block(p, 1, at.peer(at.b2)), block(p, 2, at.peer(1))]
+    for copy in sent:
+        copy.start()
+
+    def pass_on(q, slots):
+        block(q, 0, at.peer(1)).wait_recv()
+        for slot, target in slots:
+            copy = block(q, slot, target)
+            copy.start()
+            sent.append(copy)
+
+    pass_on(p ^ at.b1, [(3, at.peer(at.b2)), (4, at.peer(1))])
+    pass_on(p ^ at.b2, [(5, at.peer(1))])
+    pass_on(p ^ at.b1 ^ at.b2, [(6, at.peer(1))])
+    for bits in (1, 3, 5, 7):
+        pass_on(p ^ bits, [])
+
+    weights.second(1)
+    weights.first(2)
+    weights.third(1)
+
+    def keys_of(g):
+        return kv[:, :, g * HEAD : (g + 1) * HEAD].reshape(CLASSES * tokens, HEAD)
+
+    def values_of(g):
+        return kv[:, :, keys + g * HEAD : keys + (g + 1) * HEAD].reshape(CLASSES * tokens, HEAD)
+
+    def heads_of(ref, g):
+        return jnp.concatenate([ref[:, h * HEAD : (h + 1) * HEAD] for h in range(g * group, (g + 1) * group)], axis=0)
+
+    for g in range(KV_HEADS):
+        scores = contract(keys_of(g), heads_of(rot, g), 1, 1) * scale
+        bias = bias_ref[...]
+        scores = scores + jnp.concatenate([bias] * group, axis=1)
+        top = jnp.max(scores, axis=0, keepdims=True)
+        expo = jnp.exp(scores - top)
+        total = jnp.sum(expo, axis=0, keepdims=True)
+        chance = expo * (1.0 / total)
+        probs[g] = chance
+        mixed = contract(values_of(g), chance.astype(BF16), 0, 0)
+        turned = mixed.T.astype(BF16)
+        for h in range(group):
+            at_lane = (g * group + h) * HEAD
+            att[:, at_lane : at_lane + HEAD] = turned[h * tokens : (h + 1) * tokens]
+
+    weights.second(2)
+    weights.first(3)
+    weights.third(2)
+    weights.ready(1)
+
+    xt_ref[1] = att[...].T
+    middle = residual + jnp.dot(att[...], wa[1, :, :width], preferred_element_type=F32)
+    inverse_second = lax.rsqrt(jnp.mean(middle * middle, axis=-1, keepdims=True) + EPS)
+    normed_second = (middle * inverse_second * gains_ref[1:2, :]).astype(BF16)
+    xt_ref[2] = normed_second.T
+    for side in range(2):
+        lanes = slice(side * half, (side + 1) * half)
+        gate[:, lanes] = jnp.dot(normed_second, wa[2 + side], preferred_element_type=F32)
+    weights.second(3)
+    weights.ready(2)
+    weights.third(3)
+    for side in range(2):
+        lanes = slice(side * half, (side + 1) * half)
+        lifted[:, lanes] = jnp.dot(normed_second, wa[4 + side], preferred_element_type=F32)
+    weights.ready(3)
+
+    hidden = (gate[...] * jax.nn.sigmoid(gate[...]) * lifted[...]).astype(BF16)
+    for side in range(2):
+        dy_ref[6 + side] = jnp.concatenate(
+            [hidden[:, (2 * s + side) * high : (2 * s + side + 1) * high] for s in range(parts)], axis=1
+        )
+    out_ref[...] = (
+        middle
+        + jnp.dot(dy_ref[6], wb[0], preferred_element_type=F32)
+        + jnp.dot(dy_ref[7], wb[1], preferred_element_type=F32)
+    ).astype(BF16)
+
+    upstream = up_ref[...]
+    turned_sides = [contract(upstream, wb[side], 1, 1) for side in range(2)]
+    grad_hidden = jnp.concatenate(
+        [turned_sides[i % 2][:, (i // 2) * high : (i // 2 + 1) * high] for i in range(2 * parts)], axis=1
+    )
+    sigma = jax.nn.sigmoid(gate[...])
+    grad_gate = (grad_hidden * lifted[...] * sigma * (1.0 + gate[...] * (1.0 - sigma))).astype(BF16)
+    grad_lifted = (grad_hidden * gate[...] * sigma).astype(BF16)
+    grad_normed = jnp.zeros((tokens, width), F32)
+    for side in range(2):
+        lanes = slice(side * half, (side + 1) * half)
+        dy_ref[2 + side] = grad_gate[:, lanes]
+        dy_ref[4 + side] = grad_lifted[:, lanes]
+        grad_normed = grad_normed + contract(grad_gate[:, lanes], wa[2 + side], 1, 1)
+        grad_normed = grad_normed + contract(grad_lifted[:, lanes], wa[4 + side], 1, 1)
+
+    def norm_back(value, inverse, gain, incoming):
+        scaled = incoming * gain
+        mean = jnp.mean(scaled * value, axis=-1, keepdims=True)
+        through = inverse * scaled - value * (inverse * inverse * inverse) * mean
+        return through, jnp.sum(incoming * value * inverse, axis=0, keepdims=True)
+
+    through, gain_second = norm_back(middle, inverse_second, gains_ref[1:2, :], grad_normed)
+    gain_ref[...] = jnp.zeros_like(gain_ref)
+    gain_ref[1:2, :] = gain_second
+    grad_middle = upstream.astype(F32) + through
+    grad_branch = grad_middle.astype(BF16)
+    dy_ref[1, :, :width] = grad_branch
+    dy_ref[1, :, width:] = jnp.zeros((tokens, keys), BF16)
+    att[...] = contract(grad_branch, wa[1, :, :width], 1, 1).astype(BF16)
+
+    queries = []
+    for g in range(KV_HEADS):
+        chance = probs[g]
+        out_grad = heads_of(att, g)
+        query = heads_of(rot, g)
+        grad_probs = contract(values_of(g), out_grad, 1, 1)
+        delta = jnp.sum(grad_probs * chance, axis=0, keepdims=True)
+        grad_scores = (chance * (grad_probs - delta)).astype(BF16)
+        grad_values = jnp.dot(chance.astype(BF16), out_grad, preferred_element_type=F32)
+        grad_keys = jnp.dot(grad_scores, query, preferred_element_type=F32) * scale
+        dkv[:, :, g * HEAD : (g + 1) * HEAD] = grad_keys.reshape(CLASSES, tokens, HEAD)
+        dkv[:, :, keys + g * HEAD : keys + (g + 1) * HEAD] = grad_values.reshape(CLASSES, tokens, HEAD)
+        turned = contract(keys_of(g), grad_scores, 0, 0).T * scale
+        for h in range(group):
+            at_lane = (g * group + h) * HEAD
+            gate[:, at_lane : at_lane + HEAD] = turned[h * tokens : (h + 1) * tokens]
+
+    def halve(bit, rest, sbuf, rbuf, index):
+        copies = []
+        for i, bits in enumerate(rest):
+            sbuf[i] = dkv[p ^ bit ^ bits].astype(BF16)
+        copy = remote(sbuf, rbuf, ds.at[index], dr.at[index], at.peer(bit))
+        copy.start()
+        copy.wait()
+        for i, bits in enumerate(rest):
+            dkv[p ^ bits] = dkv[p ^ bits] + rbuf[i].astype(F32)
+
+    halve(1, (0, 2, 4, 6), c4s, c4r, 0)
+    halve(at.b1, (0, at.b2), c2s, c2r, 1)
+    halve(at.b2, (0,), c1s, c1r, 2)
+
+    gate[:, width:half] = dkv[p, :, :keys]
+    for tile, value in enumerate(turn(gate[:, :half], -1)):
+        dy_ref[0, :, tile * 128 : (tile + 1) * 128] = value.astype(BF16)
+    dy_ref[8, :, :width] = jnp.zeros((tokens, width), BF16)
+    dy_ref[8, :, width:] = dkv[p, :, keys:].astype(BF16)
+    grad_normed = contract(dy_ref[0], wa[0], 1, 1) + contract(dy_ref[8], wa[1], 1, 1)
+    through, gain_first = norm_back(residual, inverse_first, gains_ref[0:1, :], grad_normed)
+    gain_ref[0:1, :] = gain_first
+    grad_ref[...] = grad_middle + through
+
+    weights.finish()
+    for copy in sent:
+        copy.wait_send()
+
+
+def layer_pass(x, up, gains, tables, bias, wide, tall):
+    parts = lax.axis_size("fsdp")
+    tokens, width = x.shape
+    _, rows, half = wide.shape
+    high = tall.shape[1]
+    dma = pltpu.SemaphoreType.DMA
+    vm = pltpu.VMEM
+    group = HEADS // KV_HEADS
+    two = 2 * (half - width)
+    return pl.pallas_call(
+        layer_kernel,
+        out_shape=(
+            jax.ShapeDtypeStruct((tokens, width), BF16),
+            jax.ShapeDtypeStruct((tokens, width), F32),
+            jax.ShapeDtypeStruct((4, width, tokens), BF16),
+            jax.ShapeDtypeStruct((9, tokens, half), BF16),
+            jax.ShapeDtypeStruct((8, width), F32),
+        ),
+        in_specs=[VMEM] * 7 + [ANY, ANY],
+        out_specs=(VMEM,) * 5,
+        scratch_shapes=[
+            vm((WIDE, parts * rows, half), BF16),
+            vm((2, parts * high, width), BF16),
+            vm((KV_HEADS, CLASSES * tokens, group * tokens), F32),
+            vm((CLASSES, tokens, two), BF16),
+            vm((tokens, half), BF16),
+            vm((CLASSES, tokens, two), F32),
+            vm((4, tokens, two), BF16),
+            vm((4, tokens, two), BF16),
+            vm((2, tokens, two), BF16),
+            vm((2, tokens, two), BF16),
+            vm((1, tokens, two), BF16),
+            vm((1, tokens, two), BF16),
+            vm((tokens, width), BF16),
+            vm((tokens, 2 * half), F32),
+            vm((tokens, 2 * half), F32),
+            dma((2,)), dma((4, parts)), dma((4, parts)), dma((4, 2, parts)), dma((4, 4, parts)),
+            dma((4, CLASSES, parts)), dma((7,)), dma((CLASSES,)), dma((3,)), dma((3,)),
+        ],
+        compiler_params=pltpu.CompilerParams(
+            collective_id=3, has_side_effects=True, vmem_limit_bytes=62 << 20
+        ),
+        name="layer_pass",
+    )(x, up, gains, *tables, bias, wide, tall)
+
+
 def rotary_tables(positions, width):
     half = width // 2
     frequency = THETA ** (-(jnp.arange(half, dtype=jnp.float32) * 2.0 / width))
@@ -769,6 +1116,211 @@
     split = array.reshape(shape[:axis] + (parts, full) + shape[axis + 1 :])
     kept = lax.slice_in_dim(split, 0, count, axis=axis + 1)
     return kept.reshape(shape[:axis] + (parts * count,) + shape[axis + 1 :])
+
+
+def plain_layer(
+    layer_input, output_grad, wide, tall, norm_gains, block_order, sizes
+):
+    parts, width, half, kv, short, full, high = sizes
+    hidden_size = 2 * half
+    rows = layer_input.shape[1]
+    block = rows // 2
+    group = HEADS // KV_HEADS
+    scale = 1.0 / math.sqrt(HEAD)
+    ctx_place = lax.axis_index("ctx")
+    offsets = jnp.arange(block, dtype=jnp.int32)
+    own_blocks = lax.dynamic_slice_in_dim(block_order, 2 * ctx_place, 2)
+    query_pos = (own_blocks[:, None] * block + offsets[None, :]).reshape(rows)
+    key_pos = (block_order[:, None] * block + offsets[None, :]).reshape(-1)
+
+    all_wide, all_tall = gather_weights(wide, tall)
+    w_qk, w_ov, w_gate_0, w_gate_1, w_up_0, w_up_1 = [all_wide[i].reshape(width, half) for i in range(WIDE)]
+    w_down = [all_tall[i].reshape(half, width) for i in range(2)]
+
+    residual = layer_input[0].astype(jnp.float32)
+    normed_first, inverse_first = norm_forward(residual, norm_gains[0])
+    qk_pre = jnp.dot(normed_first, w_qk, preferred_element_type=jnp.float32)
+    query_pre = qk_pre[:, :width].reshape(rows, HEADS, HEAD)
+    key_pre = qk_pre[:, width:].reshape(rows, KV_HEADS, HEAD)
+    value_low = (
+        jnp.dot(normed_first, w_ov, preferred_element_type=jnp.float32)[:, width:]
+        .astype(jnp.bfloat16)
+        .reshape(rows, KV_HEADS, HEAD)
+    )
+    cosine, sine = rotary_tables(query_pos, HEAD)
+    query_rot = rotate(query_pre, cosine, sine).astype(jnp.bfloat16)
+    key_rot = rotate(key_pre, cosine, sine).astype(jnp.bfloat16)
+    keys_all, values_all = (
+        lax.all_gather(key_rot, "ctx", axis=0, tiled=True),
+        lax.all_gather(value_low, "ctx", axis=0, tiled=True),
+    )
+    keys_head = keys_all.transpose(1, 0, 2)
+    values_head = values_all.transpose(1, 0, 2)
+    queries_head = (
+        query_rot.reshape(rows, KV_HEADS, group, HEAD)
+        .transpose(1, 2, 0, 3)
+        .reshape(KV_HEADS, group * rows, HEAD)
+    )
+    row_pos = jnp.tile(query_pos, group)
+    allowed = key_pos[None, :] <= row_pos[:, None]
+
+    def head_forward(item):
+        query, key, value = item
+        scores = jnp.where(allowed, contract(query, key, 1, 1) * scale, MASKED)
+        top = jnp.max(scores, axis=-1, keepdims=True)
+        expo = jnp.exp(scores - top)
+        total = jnp.sum(expo, axis=-1, keepdims=True)
+        probs_low = (expo / total).astype(jnp.bfloat16)
+        return (
+            jnp.dot(probs_low, value, preferred_element_type=jnp.float32),
+            (top + jnp.log(total))[:, 0],
+        )
+
+    mixed, log_total = lax.map(head_forward, (queries_head, keys_head, values_head))
+    attended = (
+        mixed.reshape(KV_HEADS, group, rows, HEAD)
+        .transpose(2, 0, 1, 3)
+        .reshape(rows, HEADS * HEAD)
+        .astype(jnp.bfloat16)
+    )
+    w_out = w_ov[:, :width]
+    middle = residual + jnp.dot(attended, w_out, preferred_element_type=jnp.float32)
+    normed_second, inverse_second = norm_forward(middle, norm_gains[1])
+
+    def sides(left, right):
+        return jnp.concatenate([left, right], axis=1)
+
+    gate = sides(
+        jnp.dot(normed_second, w_gate_0, preferred_element_type=jnp.float32),
+        jnp.dot(normed_second, w_gate_1, preferred_element_type=jnp.float32),
+    )
+    lifted = sides(
+        jnp.dot(normed_second, w_up_0, preferred_element_type=jnp.float32),
+        jnp.dot(normed_second, w_up_1, preferred_element_type=jnp.float32),
+    )
+    sigma = jax.nn.sigmoid(gate)
+    hidden = (gate * sigma * lifted).astype(jnp.bfloat16)
+    hidden_split = hidden.reshape(rows, parts, 2, high)
+    hidden_sides = [hidden_split[:, :, i].reshape(rows, half) for i in range(2)]
+    layer_output = (
+        middle
+        + jnp.dot(hidden_sides[0], w_down[0], preferred_element_type=jnp.float32)
+        + jnp.dot(hidden_sides[1], w_down[1], preferred_element_type=jnp.float32)
+    ).astype(jnp.bfloat16)
+    upstream = output_grad[0]
+    grad_hidden = jnp.stack(
+        [contract(upstream, w_down[i], 1, 1).reshape(rows, parts, high) for i in range(2)], axis=2
+    ).reshape(rows, hidden_size)
+    grad_gate = (grad_hidden * lifted * sigma * (1.0 + gate * (1.0 - sigma))).astype(jnp.bfloat16)
+    grad_lifted = (grad_hidden * gate * sigma).astype(jnp.bfloat16)
+    grad_normed_second = (
+        contract(grad_gate[:, :half], w_gate_0, 1, 1)
+        + contract(grad_gate[:, half:], w_gate_1, 1, 1)
+        + contract(grad_lifted[:, :half], w_up_0, 1, 1)
+        + contract(grad_lifted[:, half:], w_up_1, 1, 1)
+    )
+    through_second, gain_second = norm_backward(
+        middle, inverse_second, norm_gains[1], grad_normed_second
+    )
+    grad_middle = upstream.astype(jnp.float32) + through_second
+    grad_branch = grad_middle.astype(jnp.bfloat16)
+    grad_attended = contract(grad_branch, w_out, 1, 1).astype(jnp.bfloat16)
+    grad_heads = (
+        grad_attended.reshape(rows, KV_HEADS, group, HEAD)
+        .transpose(1, 2, 0, 3)
+        .reshape(KV_HEADS, group * rows, HEAD)
+    )
+
+    def head_backward(item):
+        query, key, value, grad_out, log_row = item
+        scores = jnp.where(allowed, contract(query, key, 1, 1) * scale, MASKED)
+        probs = jnp.exp(scores - log_row[:, None])
+        grad_value_part = contract(probs.astype(jnp.bfloat16), grad_out, 0, 0)
+        grad_probs = contract(grad_out, value, 1, 1)
+        grad_scores = (
+            probs * (grad_probs - jnp.sum(grad_probs * probs, axis=-1, keepdims=True))
+        ).astype(jnp.bfloat16)
+        grad_query_part = jnp.dot(grad_scores, key, preferred_element_type=jnp.float32) * scale
+        grad_key_part = contract(grad_scores, query, 0, 0) * scale
+        return (grad_query_part, grad_key_part, grad_value_part)
+
+    grad_query_rot, grad_key_all, grad_value_all = lax.map(
+        head_backward, (queries_head, keys_head, values_head, grad_heads, log_total)
+    )
+    grad_key_own, grad_value_own = (
+        lax.psum_scatter(
+            grad_key_all.astype(jnp.bfloat16), "ctx", scatter_dimension=1, tiled=True
+        ).astype(jnp.float32),
+        lax.psum_scatter(
+            grad_value_all.astype(jnp.bfloat16), "ctx", scatter_dimension=1, tiled=True
+        ).astype(jnp.float32),
+    )
+    grad_query = (
+        unrotate(
+            grad_query_rot.reshape(KV_HEADS, group, rows, HEAD)
+            .transpose(2, 0, 1, 3)
+            .reshape(rows, HEADS, HEAD),
+            cosine,
+            sine,
+        )
+        .reshape(rows, HEADS * HEAD)
+        .astype(jnp.bfloat16)
+    )
+    grad_key = (
+        unrotate(grad_key_own.transpose(1, 0, 2), cosine, sine)
+        .reshape(rows, KV_HEADS * HEAD)
+        .astype(jnp.bfloat16)
+    )
+    grad_value = (
+        grad_value_own.transpose(1, 0, 2).reshape(rows, KV_HEADS * HEAD).astype(jnp.bfloat16)
+    )
+    grad_qk = sides(grad_query, grad_key)
+    zero_query = jnp.zeros((rows, width), jnp.bfloat16)
+    grad_v = sides(zero_query, grad_value)
+    grad_normed_first = contract(grad_qk, w_qk, 1, 1) + contract(grad_v, w_ov, 1, 1)
+    through_first, gain_first = norm_backward(
+        residual, inverse_first, norm_gains[0], grad_normed_first
+    )
+    input_gradient = grad_middle + through_first
+
+    xt = jnp.stack([item.T for item in (normed_first, attended, normed_second, upstream)])
+    xt = padded(xt, 1, parts, short, full)
+    dy = jnp.stack(
+        [
+            grad_qk,
+            sides(grad_branch, jnp.zeros((rows, kv), jnp.bfloat16)),
+            grad_gate[:, :half],
+            grad_gate[:, half:],
+            grad_lifted[:, :half],
+            grad_lifted[:, half:],
+            hidden_sides[0],
+            hidden_sides[1],
+            grad_v,
+        ]
+    )
+    gains = jnp.pad(jnp.stack([gain_first, gain_second]), ((0, 6), (0, 0)))
+    return layer_output, input_gradient, xt, dy, gains
+
+
+def fused_layer(
+    layer_input, output_grad, wide, tall, norm_gains, block_order, sizes
+):
+    rows = layer_input.shape[1]
+    block = rows // 2
+    ctx_place = lax.axis_index("ctx")
+    offsets = jnp.arange(block, dtype=jnp.int32)
+    own_blocks = lax.dynamic_slice_in_dim(block_order, 2 * ctx_place, 2)
+    query_pos = (own_blocks[:, None] * block + offsets[None, :]).reshape(rows)
+    key_pos = (block_order[:, None] * block + offsets[None, :]).reshape(-1)
+    bias = jnp.where(key_pos[:, None] <= query_pos[None, :], 0.0, MASKED).astype(jnp.float32)
+    lane = jnp.arange(128, dtype=jnp.int32)
+    index = (lane % (HEAD // 2)).astype(jnp.float32)
+    frequency = THETA ** (-(index * 2.0 / HEAD))
+    angle = query_pos.astype(jnp.float32)[:, None] * frequency[None, :]
+    cosine, sine = jnp.cos(angle), jnp.sin(angle)
+    early = (lane % HEAD < HEAD // 2)[None, :]
+    tables = (cosine, jnp.where(early, 0.0, sine), jnp.where(early, -sine, 0.0))
+    return layer_pass(layer_input[0], output_grad[0], norm_gains, tables, bias, wide, tall)
 
 
 def on_device(
@@ -792,23 +1344,17 @@
     gain_momentum,
     block_order,
 ):
-    rows = layer_input.shape[1]
-    block = rows // 2
-    group = HEADS // KV_HEADS
-    scale = 1.0 / math.sqrt(HEAD)
     parts = lax.axis_size("fsdp")
-    ctx_place = lax.axis_index("ctx")
     width = layer_input.shape[2]
-    hidden_size = gate_weight.shape[1]
-    half = hidden_size // 2
+    half = gate_weight.shape[1] // 2
     kv = key_weight.shape[1]
     short = width // parts
     full = -(-short // 16) * 16
     high = half // parts
-    offsets = jnp.arange(block, dtype=jnp.int32)
-    own_blocks = lax.dynamic_slice_in_dim(block_order, 2 * ctx_place, 2)
-    query_pos = (own_blocks[:, None] * block + offsets[None, :]).reshape(rows)
-    key_pos = (block_order[:, None] * block + offsets[None, :]).reshape(-1)
+    sizes = (parts, width, half, kv, short, full, high)
+
+    def sides(left, right):
+        return jnp.concatenate([left, right], axis=1)
 
     wide = jnp.stack(
         [
@@ -820,172 +1366,12 @@
             up_weight[:, half:],
         ]
     )
-    all_wide, all_tall = gather_weights(wide, down_weight.reshape(2, high, width))
-    w_qk, w_ov, w_gate_0, w_gate_1, w_up_0, w_up_1 = [all_wide[i].reshape(width, half) for i in range(WIDE)]
-    w_down = [all_tall[i].reshape(half, width) for i in range(2)]
-
-    residual = layer_input[0].astype(jnp.float32)
-    normed_first, inverse_first = norm_forward(residual, norm_gains[0])
-    qk_pre = jnp.dot(normed_first, w_qk, preferred_element_type=jnp.float32)
-    query_pre = qk_pre[:, :width].reshape(rows, HEADS, HEAD)
-    key_pre = qk_pre[:, width:].reshape(rows, KV_HEADS, HEAD)
-    value_low = (
-        jnp.dot(normed_first, w_ov, preferred_element_type=jnp.float32)[:, width:]
-        .astype(jnp.bfloat16)
-        .reshape(rows, KV_HEADS, HEAD)
-    )
-    cosine, sine = rotary_tables(query_pos, HEAD)
-    query_rot = rotate(query_pre, cosine, sine).astype(jnp.bfloat16)
-    key_rot = rotate(key_pre, cosine, sine).astype(jnp.bfloat16)
-    keys_all, values_all = (
-        lax.all_gather(key_rot, "ctx", axis=0, tiled=True),
-        lax.all_gather(value_low, "ctx", axis=0, tiled=True),
-    )
-    keys_head = keys_all.transpose(1, 0, 2)
-    values_head = values_all.transpose(1, 0, 2)
-    queries_head = (
-        query_rot.reshape(rows, KV_HEADS, group, HEAD)
-        .transpose(1, 2, 0, 3)
-        .reshape(KV_HEADS, group * rows, HEAD)
-    )
-    row_pos = jnp.tile(query_pos, group)
-    allowed = key_pos[None, :] <= row_pos[:, None]
-
-    def head_forward(item):
-        query, key, value = item
-        scores = jnp.where(allowed, contract(query, key, 1, 1) * scale, MASKED)
-        top = jnp.max(scores, axis=-1, keepdims=True)
-        expo = jnp.exp(scores - top)
-        total = jnp.sum(expo, axis=-1, keepdims=True)
-        probs_low = (expo / total).astype(jnp.bfloat16)
-        return (
-            jnp.dot(probs_low, value, preferred_element_type=jnp.float32),
-            (top + jnp.log(total))[:, 0],
-        )
-
-    mixed, log_total = lax.map(head_forward, (queries_head, keys_head, values_head))
-    attended = (
-        mixed.reshape(KV_HEADS, group, rows, HEAD)
-        .transpose(2, 0, 1, 3)
-        .reshape(rows, HEADS * HEAD)
-        .astype(jnp.bfloat16)
-    )
-    w_out = w_ov[:, :width]
-    middle = residual + jnp.dot(attended, w_out, preferred_element_type=jnp.float32)
-    normed_second, inverse_second = norm_forward(middle, norm_gains[1])
-
-    def sides(left, right):
-        return jnp.concatenate([left, right], axis=1)
-
-    gate = sides(
-        jnp.dot(normed_second, w_gate_0, preferred_element_type=jnp.float32),
-        jnp.dot(normed_second, w_gate_1, preferred_element_type=jnp.float32),
-    )
-    lifted = sides(
-        jnp.dot(normed_second, w_up_0, preferred_element_type=jnp.float32),
-        jnp.dot(normed_second, w_up_1, preferred_element_type=jnp.float32),
-    )
-    sigma = jax.nn.sigmoid(gate)
-    hidden = (gate * sigma * lifted).astype(jnp.bfloat16)
-    hidden_split = hidden.reshape(rows, parts, 2, high)
-    hidden_sides = [hidden_split[:, :, i].reshape(rows, half) for i in range(2)]
-    layer_output = (
-        middle
-        + jnp.dot(hidden_sides[0], w_down[0], preferred_element_type=jnp.float32)
-        + jnp.dot(hidden_sides[1], w_down[1], preferred_element_type=jnp.float32)
-    ).astype(jnp.bfloat16)
-    upstream = output_grad[0]
-    grad_hidden = jnp.stack(
-        [contract(upstream, w_down[i], 1, 1).reshape(rows, parts, high) for i in range(2)], axis=2
-    ).reshape(rows, hidden_size)
-    grad_gate = (grad_hidden * lifted * sigma * (1.0 + gate * (1.0 - sigma))).astype(jnp.bfloat16)
-    grad_lifted = (grad_hidden * gate * sigma).astype(jnp.bfloat16)
-    grad_normed_second = (
-        contract(grad_gate[:, :half], w_gate_0, 1, 1)
-        + contract(grad_gate[:, half:], w_gate_1, 1, 1)
-        + contract(grad_lifted[:, :half], w_up_0, 1, 1)
-        + contract(grad_lifted[:, half:], w_up_1, 1, 1)
-    )
-    through_second, gain_second = norm_backward(
-        middle, inverse_second, norm_gains[1], grad_normed_second
-    )
-    grad_middle = upstream.astype(jnp.float32) + through_second
-    grad_branch = grad_middle.astype(jnp.bfloat16)
-    grad_attended = contract(grad_branch, w_out, 1, 1).astype(jnp.bfloat16)
-    grad_heads = (
-        grad_attended.reshape(rows, KV_HEADS, group, HEAD)
-        .transpose(1, 2, 0, 3)
-        .reshape(KV_HEADS, group * rows, HEAD)
-    )
-
-    def head_backward(item):
-        query, key, value, grad_out, log_row = item
-        scores = jnp.where(allowed, contract(query, key, 1, 1) * scale, MASKED)
-        probs = jnp.exp(scores - log_row[:, None])
-        grad_value_part = contract(probs.astype(jnp.bfloat16), grad_out, 0, 0)
-        grad_probs = contract(grad_out, value, 1, 1)
-        grad_scores = (
-            probs * (grad_probs - jnp.sum(grad_probs * probs, axis=-1, keepdims=True))
-        ).astype(jnp.bfloat16)
-        grad_query_part = jnp.dot(grad_scores, key, preferred_element_type=jnp.float32) * scale
-        grad_key_part = contract(grad_scores, query, 0, 0) * scale
-        return (grad_query_part, grad_key_part, grad_value_part)
-
-    grad_query_rot, grad_key_all, grad_value_all = lax.map(
-        head_backward, (queries_head, keys_head, values_head, grad_heads, log_total)
-    )
-    grad_key_own, grad_value_own = (
-        lax.psum_scatter(
-            grad_key_all.astype(jnp.bfloat16), "ctx", scatter_dimension=1, tiled=True
-        ).astype(jnp.float32),
-        lax.psum_scatter(
-            grad_value_all.astype(jnp.bfloat16), "ctx", scatter_dimension=1, tiled=True
-        ).astype(jnp.float32),
-    )
-    grad_query = (
-        unrotate(
-            grad_query_rot.reshape(KV_HEADS, group, rows, HEAD)
-            .transpose(2, 0, 1, 3)
-            .reshape(rows, HEADS, HEAD),
-            cosine,
-            sine,
-        )
-        .reshape(rows, HEADS * HEAD)
-        .astype(jnp.bfloat16)
-    )
-    grad_key = (
-        unrotate(grad_key_own.transpose(1, 0, 2), cosine, sine)
-        .reshape(rows, KV_HEADS * HEAD)
-        .astype(jnp.bfloat16)
-    )
-    grad_value = (
-        grad_value_own.transpose(1, 0, 2).reshape(rows, KV_HEADS * HEAD).astype(jnp.bfloat16)
-    )
-    grad_qk = sides(grad_query, grad_key)
-    zero_query = jnp.zeros((rows, width), jnp.bfloat16)
-    grad_v = sides(zero_query, grad_value)
-    grad_normed_first = contract(grad_qk, w_qk, 1, 1) + contract(grad_v, w_ov, 1, 1)
-    through_first, gain_first = norm_backward(
-        residual, inverse_first, norm_gains[0], grad_normed_first
-    )
-    input_gradient = (grad_middle + through_first)[None]
-
-    xt = jnp.stack([item.T for item in (normed_first, attended, normed_second, upstream)])
-    xt = padded(xt, 1, parts, short, full)
-    dy = jnp.stack(
-        [
-            grad_qk,
-            sides(grad_branch, jnp.zeros((rows, kv), jnp.bfloat16)),
-            grad_gate[:, :half],
-            grad_gate[:, half:],
-            grad_lifted[:, :half],
-            grad_lifted[:, half:],
-            hidden_sides[0],
-            hidden_sides[1],
-            grad_v,
-        ]
-    )
-    gains = jnp.pad(jnp.stack([gain_first, gain_second]), ((0, 6), (0, 0)))
+    tall = down_weight.reshape(2, high, width)
+    fused = lax.axis_size("ctx") == CLASSES and short == full and layer_input.shape[1] == 128
+    layer = fused_layer if fused else plain_layer
+    layer_output, input_gradient, xt, dy, gains = layer(
+        layer_input, output_grad, wide, tall, norm_gains, block_order, sizes
+    )
 
     def pad_rows(array):
         return padded(array, 0, 1, short, full)
@@ -1054,7 +1440,7 @@
     new_gains = gain_shard - GAIN_RATE * gain_moment
     return (
         layer_output[None],
-        input_gradient,
+        input_gradient[None],
         *gradients,
         gain_gradient,
         *moments,

time: 784 us -> 509 us (0.65)
  matrix products: 80.1 us -> 0 us
  local copies, waits for them, and re-layouts: 113 us -> 35.3 us
  Pallas kernels: 455 us -> 425 us
  waiting for transfers between devices: 25.9 us -> 0 us
  blocking collectives: 23.7 us -> 0 us
  other arithmetic: 57.2 us -> 39.4 us
  between operations: 15.3 us -> 1.3 us
    dot_general x53 -> x0, matrix products: 80.1 us -> none  [the longest x34 52.4 us: contract(): lax.dot_general(left, right, (((left_dim,), (right_dim,)), ((), ())), pre...]
    pallas_call x1, Pallas kernels: 158 us -> 126 us  [layer_pass(): pl.pallas_call(layer_kernel, out_shape=(jax.ShapeDtypeStruct((tokens, wid...]
    unnamed x4 -> x0, waiting for transfers between devices: 25.9 us -> none
    unnamed x193 -> x62, local copies, waits for them, and re-layouts: 55.9 us -> 31.2 us
    all_gather x2 -> x0, blocking collectives: 23.7 us -> none  [the longest x1 13.4 us: on_device(): lax.all_gather(value_low, 'ctx', axis=0, tiled=True)]
    slice x9 -> x0, local copies, waits for them, and re-layouts: 17 us -> none  [the longest x1 10.2 us: on_device(): all_wide[i].reshape(width, half)]
    dot_general x4 -> x0, local copies, waits for them, and re-layouts: 8.69 us -> none  [the longest x1 2.2 us: on_device(): jnp.dot(normed_second, w_up_0, preferred_element_type=jnp.float32)]
  transfers between devices with their start and end apart: 2 -> 0, of which waited for: 1 -> 0; matrix products, arithmetic and copies ran while one was open for 6% -> 0% of each run, Pallas kernels for 0% -> 0%
where the time goes in v2:
time: 509 us; the launch traced here: 501 us
  Pallas kernels  425 us (83%)
  other arithmetic  39.4 us (8%)
  local copies, waits for them, and re-layouts  35.3 us (7%)
    pallas_call x1, Pallas kernels, reduce_gradients(): pl.pallas_call(functools.partial(reduce_kernel, parts, extra, high), out_...  194 us
    pallas_call x1, Pallas kernels, layer_pass(): pl.pallas_call(layer_kernel, out_shape=(jax.ShapeDtypeStruct((tokens, wid...  126 us
    pallas_call x1, Pallas kernels, orthogonalize(): pl.pallas_call(functools.partial(ortho_kernel, parts, rows, high, narrow)...  105 us
    unnamed x62, local copies, waits for them, and re-layouts  31.2 us
    add x5, other arithmetic, on_device(): moments = [MOMENTUM * old + new for old, new in zip(olds, gradients)]  13.5 us
    add x5, other arithmetic, on_device(): old_weights[index].astype(jnp.float32)  10.2 us

profile of v2, /device:TPU:0, one launch (start us, length us, event | category | flops | bytes accessed | tf_op | source)
XLA Modules:
  0.0 500.6 jit_solution(2739533360328165006)
XLA Ops:
  2.5 1.7 copy.47
  4.3 1.7 copy.48
  7.0 1.8 copy.45
  8.8 1.9 copy.46
  10.6 1.9 copy.50
  14.4 1.9 copy.49
  16.3 3.3 pad_maximum_fusion
  19.6 2.4 copy.52.m_down
  23.0 2.0 fusion.1
  28.5 126.3 %layer_pass.1 = (bf16[128,960]{1,0:T(8,128)(2,1)}, f32[128,960]{1,0:T(8,128)}, bf16[4,960,128]{2,1,0:T(8,128)(2,1)}, bf16[9,128,1280]{2,1,0:T(8,128)(2,1)}, f32[8,960]{1,0:T(8,128)}) custom-call(bf16[128,960]{1,0:T(8,128)(2,1)} %bitcast.69, bf16[128,960]{1,0:T(8,128)(2,1)} %bitcast.70, f32[2,960]{1,0:T(2,128)} %gains_ref.1, ...), custom_call_target="tpu_custom_call" | custom-call | tf_op jit(solution)/shard_map/layer_pass/pallas_call | solution.py:1029
  154.8 1.8 copy.59
  156.6 2.0 copy.60
  158.7 193.8 %reduce_gradients.1 = (bf16[6,240,1280]{2,1,0:T(8,128)(2,1)}, bf16[2,320,960]{2,1,0:T(8,128)(2,1)}, bf16[960,1280]{1,0:T(8,128)(2,1)}, bf16[1280,960]{1,0:T(8,128)(2,1)}, f32[8,960]{1,0:T(8,128)}) custom-call(bf16[4,960,128]{2,1,0:T(8,128)(2,1)} %get-tuple-element.40.xt_in, bf16[9,128,1280]{2,1,0:T(8,128)(2,1)} %get-tuple-element.41.dy_in, ...), custom_call_target="tpu_custom_call" | custom-call | tf_op jit(solution)/shard_map/reduce_gradients/pallas_call | solution.py:505
  362.1 2.0 copy.63
  364.1 4.3 multiply_add_fusion.2
  369.9 2.2 multiply_add_fusion.5
  372.8 2.9 multiply_add_fusion.3
  375.7 2.9 multiply_add_fusion.4
  378.7 104.5 %orthogonalize.1 = (bf16[6,240,1280]{2,1,0:T(8,128)(2,1)}, bf16[2,320,960]{2,1,0:T(8,128)(2,1)}) custom-call(bf16[960,1280]{1,0:T(8,128)(2,1)} %get-tuple-element.46.s_a, bf16[1280,960]{1,0:T(8,128)(2,1)} %get-tuple-element.47.s_b), custom_call_target="tpu_custom_call" | custom-call | tf_op jit(solution)/shard_map/orthogonalize/pallas_call | solution.py:690
  486.1 1.7 convert_multiply_fusion
  487.8 2.0 copy.58
  489.9 3.8 convert_add_fusion
  496.5 1.8 multiply_add_fusion
  498.4 1.8 multiply_add_fusion.1
  (74 shorter events, 26.8 us)
Async XLA Ops:
  0.7 13.7 %copy-start.3 = (bf16[640,960]{0,1:T(8,128)(2,1)S(1)}, bf16[640,960]{0,1:T(8,128)(2,1)}, u32[]{:S(2)}) copy-start(bf16[640,960]{0,1:T(8,128)(2,1)} %param.27) | copy-start | bytes 3686404
  0.7 11.8 %copy-start.19 = (f32[240,320]{0,1:T(8,128)S(1)}, f32[240,320]{0,1:T(8,128)}, u32[]{:S(2)}) copy-start(f32[240,320]{0,1:T(8,128)} %param.31) | copy-start | bytes 921604
  8.8 7.5 %copy-start.10 = (f32[240,960]{1,0:T(8,128)S(1)}, f32[240,960]{1,0:T(8,128)}, u32[]{:S(2)}) copy-start(f32[240,960]{1,0:T(8,128)} %param.32) | copy-start | bytes 2764804
  16.3 3.3 copy-start
  19.6 2.4 copy-start.15
  19.6 2.4 copy-start.17
  19.6 3.4 copy-start.18
  22.0 3.0 copy-start.6
  22.0 4.7 copy-start.4
  158.7 193.8 %copy-start.13 = (f32[240,320]{1,0:T(8,128)S(1)}, f32[240,320]{1,0:T(8,128)}, u32[]{:S(2)}) copy-start(f32[240,320]{1,0:T(8,128)} %copy.50) | copy-start | bytes 921604
  158.7 193.8 %copy-start.14 = (f32[240,320]{1,0:T(8,128)S(1)}, f32[240,320]{1,0:T(8,128)}, u32[]{:S(2)}) copy-start(f32[240,320]{1,0:T(8,128)} %copy.51) | copy-start | bytes 921604
  352.4 2.9 copy-start.20
  364.1 4.3 copy-start.8
  368.4 1.2 copy-start.11
  368.4 1.5 copy-start.12
  369.9 2.9 copy-start.1
  372.8 2.9 copy-start.2
  489.9 3.8 copy-start.9
  489.9 3.8 copy-start.16
  495.3 1.3 copy-start.5
  496.5 1.8 copy-start.7
